TPU v7x, 32 devices: a whole 2x2x4 slice. The times are simulated.
32 devices in a mesh: groups: 2 (over x), ctx: 8 (over z, y), tp: 2 (over core).
Axes of the slice: x: 2, y: 2, z: 4, core: 2. Of those that a mesh axis runs over, the one named last changes fastest.
Arguments:
- hyena_in: bfloat16 [3, 2048, 4096], P(None, ('groups', 'ctx'), 'tp'), parts along dimension 1, may hold values from -6 to 6
- short_filter: float32 [3, 7, 4096], P(None, None, 'tp'), may hold values from -2 to 2
- mr_taps: float32 [256, 128], P('tp'), may hold values from -0.6 to 0.6
- mr_decay: float32 [256], P('tp'), may hold values from 0.005 to 0.1
- skip: float32 [4096], P('tp'), may hold values from -6 to 6
- qkv: bfloat16 [3, 2048, 2048], P(None, ('groups', 'ctx'), 'tp'), parts along dimension 1, may hold values from -8 to 8
Outputs:
- hyena_out: bfloat16 [2048, 4096], P(('groups', 'ctx'), 'tp'), parts along dimension 0
- attn_out: bfloat16 [2048, 2048], P(('groups', 'ctx'), 'tp'), parts along dimension 0
There are 2 independent parts, one for each index of `groups`. A program takes and returns all parts, laid end to end along the dimension named above; an argument that names none is the same for every part. Nothing has to cross between parts.
All inputs are finite; a program needn't handle non-finite values.
Results may differ from a plain program's by a relative error of at most 0.008.
Values may be sent and summed in bfloat16 or wider, within the bound.
No kernel may reach another device: no remote copies, remote signals or barrier semaphores. Data moves between devices by JAX's collectives and lax.ppermute only.
A program may use at most 192 MiB of HBM per device.

v0:
```python
import math

import jax
import jax.numpy as jnp
from jax import lax
from jax.sharding import PartitionSpec as P

HEAD = 128
GW = 16


def passed_along(block, axis, distance):
    devices = range(lax.axis_size(axis))
    route = [(i - distance, i) for i in devices if i - distance in devices]
    return lax.ppermute(block, axis, route)


def short_mix(inputs, filters_in, out_count):
    short_len = filters_in.shape[1]
    accum = jnp.zeros((inputs.shape[0], out_count, inputs.shape[2]), jnp.float32)
    for tap_index in range(short_len):
        offset = short_len - 1 - tap_index
        accum = accum + filters_in[:, tap_index][:, None, :] * inputs[
            :, offset : offset + out_count
        ].astype(jnp.float32)
    return accum.astype(jnp.bfloat16)


def long_conv(mixed_ext, chan_taps, tok_rows):
    tap_count = chan_taps.shape[0]
    wide_rows = mixed_ext.astype(jnp.float32)
    accum = jnp.zeros((tok_rows, wide_rows.shape[1]), jnp.float32)
    for tap_index in range(tap_count):
        offset = tap_count - 1 - tap_index
        accum = accum + chan_taps[tap_index][None, :] * wide_rows[offset : offset + tok_rows]
    return accum


def attend_block(state_now, block_pair, queries, query_pos, score_scale):
    running_max, running_sum, accum = state_now
    key_count = block_pair.shape[1]
    head_count = queries.shape[1] // HEAD
    key_pos = jnp.arange(key_count, dtype=jnp.int32)
    causal_mask = key_pos[None, :] <= query_pos[:, None]
    max_list = []
    sum_list = []
    acc_list = []
    for head_index in range(head_count):
        low_col = head_index * HEAD
        query_head = queries[:, low_col : low_col + HEAD]
        key_head = block_pair[0][:, low_col : low_col + HEAD]
        value_head = block_pair[1][:, low_col : low_col + HEAD]
        scores = (
            lax.dot_general(
                query_head, key_head, (((1,), (1,)), ((), ())), preferred_element_type=jnp.float32
            )
            * score_scale
        )
        old_max = running_max[:, head_index]
        new_max = jnp.maximum(old_max, jnp.max(jnp.where(causal_mask, scores, -1e30), axis=1))
        weights = jnp.where(causal_mask, jnp.exp(scores - new_max[:, None]), 0.0)
        max_list.append(new_max)
        sum_list.append(jnp.sum(weights, axis=1))
        acc_list.append(
            jnp.dot(weights.astype(jnp.bfloat16), value_head, preferred_element_type=jnp.float32)
        )
    return (jnp.stack(max_list, 1), jnp.stack(sum_list, 1), jnp.concatenate(acc_list, 1))


def shards(hyena_in, short_filter, mr_taps, mr_decay, skip, qkv):
    tok_rows = hyena_in.shape[1]
    tap_count = mr_taps.shape[1]
    short_len = short_filter.shape[1]
    edge_rows = passed_along(hyena_in[:, tok_rows - (short_len - 1) :, :], "ctx", 1)
    extended = jnp.concatenate([edge_rows, hyena_in], 1)
    short_out = short_mix(extended, short_filter, tok_rows)
    mixed_rows = (short_out[0].astype(jnp.float32) * short_out[2].astype(jnp.float32)).astype(
        jnp.bfloat16
    )
    rim_pieces = []
    need_rows = min(tok_rows, tap_count - 1)
    rim_pieces.insert(0, passed_along(mixed_rows[tok_rows - need_rows :], "ctx", 1))
    mixed_ext = jnp.concatenate(rim_pieces + [mixed_rows], 0)
    gate_rows = short_out[1]
    group_count = mr_taps.shape[0]
    tap_pos = jnp.arange(tap_count, dtype=jnp.float32)
    filters_t = mr_taps.T * jnp.exp(-tap_pos[:, None] * mr_decay[None, :])
    chan_taps = jnp.broadcast_to(filters_t[:, :, None], (tap_count, group_count, GW)).reshape(
        tap_count, group_count * GW
    )
    conv_out = long_conv(mixed_ext, chan_taps, tok_rows)
    hyena_out = (
        gate_rows.astype(jnp.float32) * (conv_out + skip[None, :] * mixed_rows.astype(jnp.float32))
    ).astype(jnp.bfloat16)
    head_count = qkv.shape[2] // HEAD
    queries = qkv[0]
    first_pos = lax.axis_index("ctx") * tok_rows
    query_pos = first_pos + jnp.arange(tok_rows, dtype=jnp.int32)
    score_scale = 1.0 / math.sqrt(HEAD)

    def plain_fold(state_now, block_pair):
        return attend_block(state_now, block_pair, queries, query_pos, score_scale)

    initial = (
        jnp.full((tok_rows, head_count), -1e30, jnp.float32),
        jnp.zeros((tok_rows, head_count), jnp.float32),
        jnp.zeros((tok_rows, head_count * HEAD), jnp.float32),
    )
    block_pair = lax.all_gather(qkv[1:3], "ctx", axis=1, tiled=True)
    final_max, final_sum, final_acc = lax.cond(
        jnp.int32(0) > first_pos + tok_rows - 1,
        lambda: initial,
        lambda: plain_fold(initial, block_pair),
    )
    attn_out = (
        (final_acc.reshape(tok_rows, head_count, HEAD) / final_sum[:, :, None])
        .reshape(tok_rows, head_count * HEAD)
        .astype(jnp.bfloat16)
    )
    return (hyena_out, attn_out)


def solution(mesh):
    placed = (
        P(None, ("groups", "ctx"), "tp"),
        P(None, None, "tp"),
        P("tp", None),
        P("tp"),
        P("tp"),
        P(None, ("groups", "ctx"), "tp"),
    )
    return jax.shard_map(
        shards,
        mesh=mesh,
        in_specs=placed,
        out_specs=(P(("groups", "ctx"), "tp"), P(("groups", "ctx"), "tp")),
        check_vma=False,
    )
```

profile of v0, /device:TPU:0, one launch (start us, length us, event | category | flops | bytes accessed | tf_op | source)
XLA Modules:
  0.0 133.4 jit_solution(14763192153401399072)
XLA Ops:
  7.2 0.9 slice.1438
  8.1 4.9 %collective-permute-start = (bf16[3,6,2048]{2,1,0:T(8,128)(2,1)S(1)}, bf16[3,6,2048]{2,1,0:T(8,128)(2,1)S(1)}, u32[]{:S(2)}, u32[]{:S(2)}) collective-permute-start(bf16[3,6,2048]{2,1,0:T(8,128)(2,1)S(1)} %slice.1438), channel_id=1, source_target_pairs={{0,2},{2,4},{4,6},{6,8},{8,10},{10,12},{12,14},{1,3},{3,5},{5,7},{... | collective-permute-start | bytes 221192 | tf_op jit(solution)/shard_map/ppermute | solution.py:15
  13.0 1.9 %slice.1839 = bf16[2,128,1024]{2,1,0:T(8,128)(2,1)} slice(bf16[3,128,1024]{2,1,0:T(8,128)(2,1)} %param.13), slice={[1:3], [0:128], [0:1024]} | slice | bytes 1048576 | tf_op jit(solution)/shard_map/slice | solution.py:109
  14.9 0.9 bitcast_multiply_fusion
  15.9 1.3 slice_reduce_fusion.127
  17.1 0.8 slice_reduce_fusion.126
  17.9 0.8 slice_reduce_fusion.125
  18.7 0.8 slice_reduce_fusion.124
  19.5 0.8 slice_reduce_fusion.123
  20.6 0.8 slice_reduce_fusion.122
  21.4 3.0 %add_convert_fusion = bf16[3,128,2048]{2,1,0:T(8,128)(2,1)S(1)} fusion(bf16[3,128,2048]{2,1,0:T(8,128)(2,1)S(1)} %copy-done.2, bf16[3,6,2048]{2,1,0:T(8,128)(2,1)S(1)} %collective-permute-done, f32[3,2048]{1,0:T(4,128)S(1)} %get-tuple-element.185, f32[3,2048]{1,0:T(4,128)S(1)} %get-tuple-element.186, f32[3,2048]{1,0:T(4,128)S(1)} %get-tuple-element.187, ...), kind=kLoop, calls=%fused_computation.122 | loop fusion | flops 30670848 | bytes 3391488 | tf_op jit(solution)/shard_map/convert_element_type | solution.py:26
  24.6 3.6 %collective-permute-start.1 = (bf16[127,2048]{1,0:T(8,128)(2,1)S(1)}, bf16[127,2048]{1,0:T(8,128)(2,1)S(1)}, u32[]{:S(2)}, u32[]{:S(2)}) collective-permute-start(bf16[127,2048]{1,0:T(8,128)(2,1)S(1)} %slice_bitcast_fusion.3), channel_id=1, source_target_pairs={{0,2},{2,4},{4,6},{6,8},{8,10},{10,12},{12,14},{1,3},{3,5},{5,7},{... | collective-permute-start | bytes 1560584 | tf_op jit(solution)/shard_map/ppermute | solution.py:15
  28.3 1.2 slice_reduce_fusion.121
  48.0 0.7 broadcast_in_dim.798
  48.7 0.7 broadcast_in_dim.799
  50.1 0.7 broadcast_in_dim.801
  52.9 0.7 broadcast_in_dim.805
  55.7 0.7 broadcast_in_dim.809
  56.4 0.7 broadcast_in_dim.810
  57.1 0.7 broadcast_in_dim.811
  57.9 0.7 broadcast_in_dim.812
  58.6 0.7 broadcast_in_dim.569
  59.9 0.7 broadcast_in_dim.571
  60.7 0.7 broadcast_in_dim.572
  61.4 0.7 broadcast_in_dim.573
  62.8 0.7 broadcast_in_dim.575
  65.6 0.7 broadcast_in_dim.579
  68.3 0.8 broadcast_in_dim.583
  69.7 0.7 broadcast_in_dim.585
  71.1 0.7 broadcast_in_dim.587
  71.9 0.7 broadcast_in_dim.588
  73.9 0.7 broadcast_in_dim.591
  76.0 0.7 broadcast_in_dim.594
  79.1 27.0 %fusion.88 = bf16[128,2048]{1,0:T(8,128)(2,1)} fusion(f32[255,2048]{1,0:T(8,128)S(1)} %maximum_convert_fusion, f32[2048]{0:T(1024)S(1)} %copy-done.26, f32[2048]{0:T(1024)S(1)} %copy-done.11, f32[2048]{0:T(1024)S(1)} %copy-done.10, f32[2048]{0:T(1024)S(1)} %copy-done.9, f32[2048]{0:T(1024)S(1)} %copy-done.8, f32[2048]{0:T(1024)S(1)} %copy-done.7, ...), kind=kLoop, calls=%fused_computation.136 | loop fusion | flops 69468160 | bytes 137371648 | tf_op jit(solution)/shard_map/convert_element_type | solution.py:94
  106.1 18.3 %conditional.1 = (f32[128,8]{0,1:T(8,128)S(1)}, f32[128,1024]{1,0:T(8,128)}) conditional(s32[]{:T(128)} %convert_element_type.100, (s32[]{:T(128)}, s32[128]{0:T(128)S(1)}, bf16[3,128,1024]{2,1,0:T(8,128)(2,1)}, bf16[2,1024,1024]{2,1,0:T(8,128)(2,1)}) %tuple.16, () %tuple.17), branch_computations={%region_0.17_spmd, %region_17.18_spmd} | conditional | flops 547617920 | bytes 35428428 | solution.py:110
  106.1 2.7 %slice_bitcast_fusion = (bf16[1024,1024]{1,0:T(8,128)(2,1)S(1)}, bf16[1024,1024]{1,0:T(8,128)(2,1)S(1)}) fusion(bf16[2,1024,1024]{2,1,0:T(8,128)(2,1)} %get-tuple-element.15), kind=kLoop, calls=%fused_computation | loop fusion | bytes 8388608 | tf_op jit(solution)/shard_map/cond/branch_0_fun/squeeze | solution.py:52
  108.7 1.0 slice_bitcast_fusion.2
  112.3 1.0 convolution_dynamic-update-slice_fusion.7
  113.3 1.0 convolution_dynamic-update-slice_fusion.6
  114.3 1.0 convolution_dynamic-update-slice_fusion.5
  115.2 1.0 convolution_dynamic-update-slice_fusion.4
  116.2 1.0 convolution_dynamic-update-slice_fusion.3
  117.2 1.0 convolution_dynamic-update-slice_fusion.2
  118.1 1.0 convolution_dynamic-update-slice_fusion.1
  119.1 1.0 convolution_dynamic-update-slice_fusion
  120.1 2.0 %copy.12 = f32[128,1024]{1,0:T(8,128)} copy(f32[128,1024]{0,1:T(8,128)} %convolution_dynamic-update-slice_fusion) | data formatting | bytes 1048576 | tf_op jit(solution)/shard_map/cond | solution.py:110
  122.1 2.2 %fusion.15 = (f32[128]{0:T(128)S(1)}, f32[128]{0:T(128)S(1)}, f32[128]{0:T(128)S(1)}, f32[128]{0:T(128)S(1)}, f32[128]{0:T(128)S(1)}, /*index=5*/f32[128]{0:T(128)S(1)}, f32[128]{0:T(128)S(1)}, f32[128]{0:T(128)S(1)}) fusion(f32[128,1024]{1,0:T(8,128)} %copy-done.1, f32[128]{0:T(128)S(1)} %get-tuple-element.170, s32[128]{0:T(128)S(1)} %broadcast_add_fusion, ...), kind=kLoop, calls=%fused_computation.50 | loop fusion | flops 3275776 | bytes 4203008 | tf_op jit(solution)/shard_map/cond/branch_0_fun/reduce_sum | solution.py:63
  124.7 1.9 %fusion.215 = bf16[128,1024]{1,0:T(8,128)(2,1)} fusion(f32[128,1024]{1,0:T(8,128)} %get-tuple-element.22, f32[16,8,8,128]{3,2,1,0:T(8,128)S(1)} %bitcast.46), kind=kLoop, calls=%fused_computation.394 | loop fusion | flops 262144 | bytes 1310720 | tf_op jit(solution)/shard_map/convert_element_type | solution.py:118
  (322 shorter events, 38.4 us)
Async XLA Ops:
  7.2 98.9 %all-gather.2.cloned.1.call-start = ((), (), s32[]{:S(2)}) async-start(), calls=%async_computation | async-start | bytes 4718592 | tf_op jit(solution)/shard_map/all_gather | solution.py:109
  8.1 13.2 %collective-permute-start = (bf16[3,6,2048]{2,1,0:T(8,128)(2,1)S(1)}, bf16[3,6,2048]{2,1,0:T(8,128)(2,1)S(1)}, u32[]{:S(2)}, u32[]{:S(2)}) collective-permute-start(bf16[3,6,2048]{2,1,0:T(8,128)(2,1)S(1)} %slice.1438), channel_id=1, source_target_pairs={{0,2},{2,4},{4,6},{6,8},{8,10},{10,12},{12,14},{1,3},{3,5},{5,7},{... | collective-permute-start | bytes 221192 | tf_op jit(solution)/shard_map/ppermute | solution.py:15
  17.9 2.4 %copy-start.3 = (f32[3,7,2048]{2,1,0:T(8,128)S(1)}, f32[3,7,2048]{2,1,0:T(8,128)}, u32[]{:S(2)}) copy-start(f32[3,7,2048]{2,1,0:T(8,128)} %param.9) | copy-start | bytes 516100
  18.7 2.6 %copy-start.2 = (bf16[3,128,2048]{2,1,0:T(8,128)(2,1)S(1)}, bf16[3,128,2048]{2,1,0:T(8,128)(2,1)}, u32[]{:S(2)}) copy-start(bf16[3,128,2048]{2,1,0:T(8,128)(2,1)} %param.8) | copy-start | bytes 4718596
  24.6 53.8 %collective-permute-start.1 = (bf16[127,2048]{1,0:T(8,128)(2,1)S(1)}, bf16[127,2048]{1,0:T(8,128)(2,1)S(1)}, u32[]{:S(2)}, u32[]{:S(2)}) collective-permute-start(bf16[127,2048]{1,0:T(8,128)(2,1)S(1)} %slice_bitcast_fusion.3), channel_id=1, source_target_pairs={{0,2},{2,4},{4,6},{6,8},{8,10},{10,12},{12,14},{1,3},{3,5},{5,7},{... | collective-permute-start | bytes 1560584 | tf_op jit(solution)/shard_map/ppermute | solution.py:15
  78.1 0.7 copy-start.4
  78.1 0.7 copy-start.5
  78.1 0.7 copy-start.6
  78.1 0.7 copy-start.7
  78.1 0.8 copy-start.8
  78.1 0.8 copy-start.9
  78.1 0.8 copy-start.10
  78.1 0.8 copy-start.11
  78.1 0.8 copy-start.12
  78.1 0.8 copy-start.13
  78.2 0.8 copy-start.14
  78.2 0.8 copy-start.15
  78.2 0.8 copy-start.16
  78.2 0.8 copy-start.17
  78.2 0.8 copy-start.18
  78.2 0.8 copy-start.19
  78.2 0.8 copy-start.20
  78.2 0.8 copy-start.21
  78.2 0.8 copy-start.22
  78.2 0.8 copy-start.23
  78.3 0.8 copy-start.24
  78.3 0.8 copy-start.25
  78.3 0.8 copy-start.26
  111.5 0.8 copy-start
  112.2 6.9 %copy-start.1 = (f32[128,1024]{1,0:T(8,128)}, f32[128,1024]{1,0:T(8,128)S(1)}, u32[]{:S(2)}) copy-start(f32[128,1024]{1,0:T(8,128)S(1)} %get-tuple-element.169) | copy-start | bytes 1572868 | tf_op jit(solution)/shard_map/cond
Sparse Core Ops, SparseCore 0:
  15.0 83.5 all-gather.1
where the time goes:
time: 134 us; the launch traced here: 133 us
  local copies, waits for them, and re-layouts  64.6 us (48%)
  other arithmetic  35.5 us (26%)
  between operations  14.5 us (11%)
  matrix products  10.2 us (8%)
  starting transfers between devices  8.55 us (6%)
    broadcast_in_dim x256, local copies, waits for them, and re-layouts, shards(): jnp.broadcast_to(filters_t[:, :, None], (tap_count, group_count, GW))  48.5 us
    convert_element_type x1, other arithmetic, shards(): hyena_out = (gate_rows.astype(jnp.float32) * (conv_out + skip[None, :] *...  27 us
    ppermute x2, starting transfers between devices, passed_along(): return lax.ppermute(block, axis, route)  8.51 us
    dot_general x8, matrix products, attend_block(): jnp.dot(weights.astype(jnp.bfloat16), value_head, preferred_element_type=...  7.75 us
    slice x7, local copies, waits for them, and re-layouts, long_conv(): chan_taps[tap_index][None, :] * wide_rows[offset:offset + tok_rows]  6.35 us
    convert_element_type x1, other arithmetic, short_mix(): return accum.astype(jnp.bfloat16)  2.98 us
  transfers between devices with their start and end apart: 3, of which 0 were waited for; matrix products, arithmetic and copies ran while one was open for 66% of the time, Pallas kernels for 0%

commit v1 on v0

v1 whole, which is shorter than its diff:
```python
import math

import jax
import jax.numpy as jnp
from jax import lax
from jax.experimental import pallas as pl
from jax.experimental.pallas import tpu as pltpu
from jax.sharding import PartitionSpec as P

HEAD = 128
GW = 16
LANES = 128
EDGE = 8


def passed_along(block, axis, distance):
    devices = range(lax.axis_size(axis))
    route = [(i - distance, i) for i in devices if i - distance in devices]
    return lax.ppermute(block, axis, route)


def short_mix(x, edge, short_filter):
    streams, rows, width = x.shape
    taps = short_filter.shape[1]
    cols = min(512, width)

    def body(x_ref, edge_ref, filt_ref, mixed_ref, gate_ref, ext_ref):
        out = []
        for s in range(streams):
            ext_ref[s, :EDGE, :] = edge_ref[s].astype(jnp.float32)
            ext_ref[s, EDGE:, :] = x_ref[s].astype(jnp.float32)
        for c in range(cols // LANES):
            at = pl.ds(c * LANES, LANES)
            out = []
            for s in range(streams):
                accum = None
                for j in reversed(range(taps)):
                    part = filt_ref[s, j : j + 1, at] * ext_ref[s, pl.ds(EDGE - j, rows), at]
                    accum = part if accum is None else accum + part
                out.append(accum.astype(jnp.bfloat16))
            mixed_ref[:, at] = (out[0].astype(jnp.float32) * out[2].astype(jnp.float32)).astype(
                jnp.bfloat16
            )
            gate_ref[:, at] = out[1]

    return pl.pallas_call(
        body,
        name="short_mix",
        grid=(width // cols,),
        in_specs=[
            pl.BlockSpec((streams, rows, cols), lambda c: (0, 0, c)),
            pl.BlockSpec((streams, EDGE, cols), lambda c: (0, 0, c)),
            pl.BlockSpec((streams, taps, cols), lambda c: (0, 0, c)),
        ],
        out_specs=[
            pl.BlockSpec((rows, cols), lambda c: (0, c)),
            pl.BlockSpec((rows, cols), lambda c: (0, c)),
        ],
        out_shape=[jax.ShapeDtypeStruct((rows, width), jnp.bfloat16)] * 2,
        scratch_shapes=[pltpu.VMEM((streams, rows + EDGE, cols), jnp.float32)],
        cost_estimate=pl.CostEstimate(
            flops=2 * streams * taps * rows * width,
            transcendentals=0,
            bytes_accessed=10 * rows * width,
        ),
    )(x, edge, short_filter)


def long_conv(prev, mixed, gate, filters_back, skip):
    rows, width = mixed.shape
    taps = filters_back.shape[1]
    cols = min(512, width)
    per_block = LANES // GW

    def body(prev_ref, mixed_ref, gate_ref, filt_ref, skip_ref, out_ref, band_ref):
        row = lax.broadcasted_iota(jnp.int32, (rows, taps), 0)
        col = lax.broadcasted_iota(jnp.int32, (rows, taps), 1)
        lane_group = lax.broadcasted_iota(jnp.int32, (rows, LANES), 1) // GW
        for c in range(cols // LANES):
            at = pl.ds(c * LANES, LANES)
            for g in range(per_block):
                base = jnp.broadcast_to(filt_ref[pl.ds(c * per_block + g, 1), :], (rows, taps))
                ring = pltpu.roll(base, 0, 1, stride=1, stride_axis=0)
                band_ref[c, pl.ds(g * rows, rows), :taps] = jnp.where(col > row, ring, 0.0).astype(
                    jnp.bfloat16
                )
                band_ref[c, pl.ds(g * rows, rows), taps:] = jnp.where(col <= row, ring, 0.0).astype(
                    jnp.bfloat16
                )
            here = mixed_ref[:, at]
            both = jnp.concatenate([prev_ref[:, at], here], 0)
            conv_all = jnp.dot(band_ref[c], both, preferred_element_type=jnp.float32)
            conv = conv_all[:rows]
            for g in range(1, per_block):
                conv = jnp.where(lane_group == g, conv_all[g * rows : (g + 1) * rows], conv)
            out_ref[:, at] = (
                gate_ref[:, at].astype(jnp.float32)
                * (conv + skip_ref[:, at] * here.astype(jnp.float32))
            ).astype(jnp.bfloat16)

    wide = pl.BlockSpec((rows, cols), lambda c: (0, c))
    return pl.pallas_call(
        body,
        name="long_conv",
        grid=(width // cols,),
        in_specs=[
            wide,
            wide,
            wide,
            pl.BlockSpec((cols // GW, taps), lambda c: (c, 0)),
            pl.BlockSpec((1, cols), lambda c: (0, c)),
        ],
        out_specs=wide,
        out_shape=jax.ShapeDtypeStruct((rows, width), jnp.bfloat16),
        scratch_shapes=[pltpu.VMEM((cols // LANES, per_block * rows, 2 * taps), jnp.bfloat16)],
        cost_estimate=pl.CostEstimate(
            flops=2 * (width // GW) * LANES * rows * 2 * taps,
            transcendentals=0,
            bytes_accessed=10 * rows * width,
        ),
    )(prev, mixed, gate, filters_back, skip)


def head_attention(blocks, scale):
    parts, _, rows, width = blocks.shape
    step = 2 if parts % 2 == 0 else 1
    q_rows = step * rows

    def body(in_ref, out_ref):
        row = lax.broadcasted_iota(jnp.int32, (q_rows, q_rows), 0)
        col = lax.broadcasted_iota(jnp.int32, (q_rows, q_rows), 1)
        keep = col <= row
        for h in range(width // HEAD):
            at = pl.ds(h * HEAD, HEAD)
            for b in range(parts // step):
                upto = (b + 1) * step
                query = in_ref[b * step : upto, 0, :, at].reshape(q_rows, HEAD)
                keys = in_ref[:upto, 1, :, at].reshape(upto * rows, HEAD)
                values = in_ref[:upto, 2, :, at].reshape(upto * rows, HEAD)
                scores = lax.dot_general(
                    query, keys, (((1,), (1,)), ((), ())), preferred_element_type=jnp.float32
                )
                low = b * q_rows
                edge_scores = jnp.where(keep, scores[:, low:], -1e30)
                if b:
                    scores = jnp.concatenate([scores[:, :low], edge_scores], 1)
                else:
                    scores = edge_scores
                top = jnp.max(scores, axis=1, keepdims=True)
                weights = jnp.exp((scores - top) * scale)
                total = jnp.sum(weights, axis=1, keepdims=True)
                summed = jnp.dot(
                    weights.astype(jnp.bfloat16), values, preferred_element_type=jnp.float32
                )
                out_ref[b * step : upto, :, at] = (
                    (summed / total).astype(jnp.bfloat16).reshape(step, rows, HEAD)
                )

    tokens = parts * rows
    return pl.pallas_call(
        body,
        name="head_attention",
        out_shape=jax.ShapeDtypeStruct((parts, rows, width), jnp.bfloat16),
        cost_estimate=pl.CostEstimate(
            flops=2 * tokens * tokens * width,
            transcendentals=tokens * tokens * width // (2 * HEAD),
            bytes_accessed=8 * tokens * width,
        ),
    )(blocks)


def gathered_attention(qkv, scale):
    tok_rows = qkv.shape[1]
    head_count = qkv.shape[2] // HEAD
    queries = qkv[0]
    query_pos = lax.axis_index("ctx") * tok_rows + jnp.arange(tok_rows, dtype=jnp.int32)
    block_pair = lax.all_gather(qkv[1:3], "ctx", axis=1, tiled=True)
    key_pos = jnp.arange(block_pair.shape[1], dtype=jnp.int32)
    causal_mask = key_pos[None, :] <= query_pos[:, None]
    out_list = []
    for head_index in range(head_count):
        cols = slice(head_index * HEAD, (head_index + 1) * HEAD)
        scores = (
            lax.dot_general(
                queries[:, cols],
                block_pair[0][:, cols],
                (((1,), (1,)), ((), ())),
                preferred_element_type=jnp.float32,
            )
            * scale
        )
        top = jnp.max(jnp.where(causal_mask, scores, -1e30), axis=1)
        weights = jnp.where(causal_mask, jnp.exp(scores - top[:, None]), 0.0)
        total = jnp.sum(weights, axis=1)
        summed = jnp.dot(
            weights.astype(jnp.bfloat16),
            block_pair[1][:, cols],
            preferred_element_type=jnp.float32,
        )
        out_list.append((summed / total[:, None]).astype(jnp.bfloat16))
    return jnp.concatenate(out_list, 1)


def traded_attention(qkv, scale):
    parts = lax.axis_size("ctx")
    tok_rows = qkv.shape[1]
    width = qkv.shape[2] // parts
    outgoing = qkv.reshape(3, tok_rows, parts, width).transpose(2, 0, 1, 3)
    blocks = lax.all_to_all(outgoing, "ctx", 0, 0, tiled=True)
    done = head_attention(blocks, scale)
    back = lax.all_to_all(done, "ctx", 0, 0, tiled=True)
    return back.transpose(1, 0, 2).reshape(tok_rows, parts * width)


def shards(hyena_in, short_filter, mr_taps, mr_decay, skip, qkv):
    tok_rows = hyena_in.shape[1]
    tap_count = mr_taps.shape[1]
    scale = 1.0 / math.sqrt(HEAD)
    if (qkv.shape[2] // HEAD) % lax.axis_size("ctx") == 0:
        attn_out = traded_attention(qkv, scale)
    else:
        attn_out = gathered_attention(qkv, scale)
    edge = passed_along(hyena_in[:, tok_rows - EDGE :, :], "ctx", 1)
    mixed, gate = short_mix(hyena_in, edge, short_filter)
    prev = passed_along(mixed, "ctx", 1)
    tap_pos = jnp.arange(tap_count, dtype=jnp.float32)
    filters = mr_taps * jnp.exp(-mr_decay[:, None] * tap_pos[None, :])
    filters_back = jnp.concatenate([filters[:, :1], filters[:, :0:-1]], 1)
    hyena_out = long_conv(prev, mixed, gate, filters_back, skip[None, :])
    return (hyena_out, attn_out)


def solution(mesh):
    placed = (
        P(None, ("groups", "ctx"), "tp"),
        P(None, None, "tp"),
        P("tp", None),
        P("tp"),
        P("tp"),
        P(None, ("groups", "ctx"), "tp"),
    )
    return jax.shard_map(
        shards,
        mesh=mesh,
        in_specs=placed,
        out_specs=(P(("groups", "ctx"), "tp"), P(("groups", "ctx"), "tp")),
        check_vma=False,
    )
```

time: 134 us -> 64.7 us (0.48)
  the two profiles are of different devices: /device:TPU:0 before, /device:TPU:16 now
where the time goes in v1:
time: 64.7 us; the launch traced here: 64.1 us
  waiting for transfers between devices  23.9 us (37%)
  starting transfers between devices  17.2 us (27%)
  Pallas kernels  14.3 us (22%)
  local copies, waits for them, and re-layouts  7.09 us (11%)
  other arithmetic  0.81 us (1%)
  between operations  0.71 us (1%)
    ppermute x2, waiting for transfers between devices, passed_along(): return lax.ppermute(block, axis, route)  23.9 us
    all_to_all x1, starting transfers between devices, traded_attention(): blocks = lax.all_to_all(outgoing, 'ctx', 0, 0, tiled=True)  6.17 us
    all_to_all x1, starting transfers between devices, traded_attention(): back = lax.all_to_all(done, 'ctx', 0, 0, tiled=True)  5.66 us
    pallas_call x1, Pallas kernels, short_mix(): pl.pallas_call(body, name='short_mix', grid=(width // cols,), in_specs=[p...  5.46 us
    ppermute x2, starting transfers between devices, passed_along(): return lax.ppermute(block, axis, route)  5.41 us
    pallas_call x1, Pallas kernels, long_conv(): pl.pallas_call(body, name='long_conv', grid=(width // cols,), in_specs=[w...  5.3 us
    unnamed x12, local copies, waits for them, and re-layouts  4.68 us
    pallas_call x1, Pallas kernels, head_attention(): pl.pallas_call(body, name='head_attention', out_shape=jax.ShapeDtypeStruc...  3.58 us
  transfers between devices with their start and end apart: 4, of which 2 were waited for; matrix products, arithmetic and copies ran while one was open for 3% of the time, Pallas kernels for 22%

profile of v1, /device:TPU:16, one launch (start us, length us, event | category | flops | bytes accessed | tf_op | source)
XLA Modules:
  0.0 64.1 jit_solution(16757327172849919553)
XLA Ops:
  0.6 1.5 %copy.8 = bf16[3,128,1024]{1,2,0:T(8,128)(2,1)S(1)} copy(bf16[3,128,1024]{2,1,0:T(8,128)(2,1)} %param.11) | data formatting | bytes 1572864 | tf_op args[5]
  2.1 1.2 %copy.9 = bf16[3,128,8,128]{3,1,0,2:T(8,128)(2,1)} copy(bf16[3,128,8,128]{1,3,2,0:T(8,128)(2,1)S(1)} %bitcast.6) | data formatting | bytes 1572864 | tf_op jit(solution)/shard_map/reshape | solution.py:208
  3.3 6.2 %all-to-all-start = ((bf16[8,3,128,128]{3,2,1,0:T(8,128)(2,1)}), bf16[8,3,128,128]{3,2,1,0:T(8,128)(2,1)S(1)}, u32[]{:S(2)}, u32[]{:S(2)}) async-start(bf16[8,3,128,128]{3,2,1,0:T(8,128)(2,1)} %bitcast.2), calls=%async_computation | async-start | bytes 1572864 | tf_op jit(solution)/shard_map/all_to_all | solution.py:209
  9.5 0.9 %slice.9 = bf16[3,8,2048]{2,1,0:T(8,128)(2,1)S(1)} slice(bf16[3,128,2048]{2,1,0:T(8,128)(2,1)} %x_ref.1), slice={[0:3], [120:128], [0:2048]} | slice | bytes 196608 | tf_op jit(solution)/shard_map/slice | solution.py:223
  10.4 0.0 copy-start.4
  10.4 0.0 copy-start.2
  10.4 3.5 %collective-permute-start = (bf16[3,8,2048]{2,1,0:T(8,128)(2,1)S(1)}, bf16[3,8,2048]{2,1,0:T(8,128)(2,1)S(1)}, u32[]{:S(2)}, u32[]{:S(2)}) collective-permute-start(bf16[3,8,2048]{2,1,0:T(8,128)(2,1)S(1)} %slice.9), channel_id=1, source_target_pairs={{0,2},{2,4},{4,6},{6,8},{8,10},{10,12},{12,14},{1,3},{3,5},{5,7},{... | collective-permute-start | bytes 294920 | tf_op jit(solution)/shard_map/ppermute | solution.py:19
  13.9 16.3 %collective-permute-done.edge_ref = bf16[3,8,2048]{2,1,0:T(8,128)(2,1)S(1)} collective-permute-done((bf16[3,8,2048]{2,1,0:T(8,128)(2,1)S(1)}, bf16[3,8,2048]{2,1,0:T(8,128)(2,1)S(1)}, u32[]{:S(2)}, u32[]{:S(2)}) %collective-permute-start) | collective-permute-done | bytes 98336 | tf_op jit(solution)/shard_map/ppermute | solution.py:19
  30.2 0.0 copy-start.1
  30.2 0.6 copy-done.1
  30.9 5.5 %short_mix.1 = (bf16[128,2048]{1,0:T(8,128)(2,1)}, bf16[128,2048]{1,0:T(8,128)(2,1)}) custom-call(bf16[3,128,2048]{2,1,0:T(8,128)(2,1)} %x_ref.1, bf16[3,8,2048]{2,1,0:T(8,128)(2,1)} %copy-done.1, f32[3,7,2048]{2,1,0:T(8,128)} %filt_ref.1), custom_call_target="tpu_custom_call" | custom-call | flops 11010048 | bytes 2621440 | tf_op jit(solution)/shard_map/short_mix/pallas_call | solution.py:46
  36.3 1.9 %collective-permute-start.1 = (bf16[128,2048]{1,0:T(8,128)(2,1)}, bf16[128,2048]{1,0:T(8,128)(2,1)S(1)}, u32[]{:S(2)}, u32[]{:S(2)}) collective-permute-start(bf16[128,2048]{1,0:T(8,128)(2,1)} %get-tuple-element.4.mixed_ref), channel_id=1, source_target_pairs={{0,2},{2,4},{4,6},{6,8},{8,10},{10,12},{12,14},{1,3},{3,5},{5,7},{... | collective-permute-start | bytes 1572872 | tf_op jit(solution)/shard_map/ppermute | solution.py:19
  38.3 0.0 all-to-all-done.in_ref
  38.3 0.0 copy-start
  38.3 0.9 %copy-done = bf16[8,3,128,128]{3,2,1,0:T(8,128)(2,1)} copy-done((bf16[8,3,128,128]{3,2,1,0:T(8,128)(2,1)}, bf16[8,3,128,128]{3,2,1,0:T(8,128)(2,1)S(1)}, u32[]{:S(2)}) %copy-start) | copy-done | bytes 786456
  39.2 3.6 %head_attention.1 = bf16[8,128,128]{2,1,0:T(8,128)(2,1)} custom-call(bf16[8,3,128,128]{3,2,1,0:T(8,128)(2,1)} %copy-done), custom_call_target="tpu_custom_call" | custom-call | flops 268435456 | bytes 1048576 | tf_op jit(solution)/shard_map/head_attention/pallas_call | solution.py:160
  42.7 5.7 %all-to-all-start.1 = ((bf16[8,128,128]{2,1,0:T(8,128)(2,1)}), bf16[8,128,128]{2,1,0:T(8,128)(2,1)S(1)}, u32[]{:S(2)}, u32[]{:S(2)}) async-start(bf16[8,128,128]{2,1,0:T(8,128)(2,1)} %head_attention.1), calls=%async_computation.1 | async-start | bytes 524288 | tf_op jit(solution)/shard_map/all_to_all | solution.py:211
  48.4 0.0 copy-done.4
  48.4 0.0 copy-done.2
  48.4 0.1 exponential_multiply_fusion
  48.5 0.1 slice.13
  48.6 0.1 rev.3
  48.7 0.7 %pad_maximum_fusion.filt_ref = f32[128,128]{1,0:T(8,128)} fusion(f32[128,127]{1,0:T(8,128)S(1)} %rev.3, f32[128,1]{1,0:T(8,128)S(1)} %bitcast.9), kind=kLoop, calls=%fused_computation | loop fusion | flops 16384 | bytes 131072 | tf_op jit(solution)/shard_map/concatenate | solution.py:228
  49.4 7.5 %collective-permute-done.1.prev_ref = bf16[128,2048]{1,0:T(8,128)(2,1)S(1)} collective-permute-done((bf16[128,2048]{1,0:T(8,128)(2,1)}, bf16[128,2048]{1,0:T(8,128)(2,1)S(1)}, u32[]{:S(2)}, u32[]{:S(2)}) %collective-permute-start.1) | collective-permute-done | bytes 524320 | tf_op jit(solution)/shard_map/ppermute | solution.py:19
  56.9 0.0 copy-start.3
  56.9 0.8 %copy-done.3 = bf16[128,2048]{1,0:T(8,128)(2,1)} copy-done((bf16[128,2048]{1,0:T(8,128)(2,1)}, bf16[128,2048]{1,0:T(8,128)(2,1)S(1)}, u32[]{:S(2)}) %copy-start.3) | copy-done | bytes 524312
  57.7 5.3 %long_conv.1 = bf16[128,2048]{1,0:T(8,128)(2,1)} custom-call(bf16[128,2048]{1,0:T(8,128)(2,1)} %copy-done.3, bf16[128,2048]{1,0:T(8,128)(2,1)} %get-tuple-element.4.mixed_ref, bf16[128,2048]{1,0:T(8,128)(2,1)} %get-tuple-element.5.gate_ref, f32[128,128]{1,0:T(8,128)} %pad_maximum_fusion.filt_ref, f32[1,2048]{1,0:T(1,128)} %bitcast.10), custom_call_target="tpu_custom_call" | custom-call | flops 1073741824 | bytes 2621440 | tf_op jit(solution)/shard_map/long_conv/pallas_call | solution.py:102
  63.0 0.0 all-to-all-done.1
  63.0 0.2 copy.10
  63.2 0.9 %copy.11 = bf16[128,1024]{1,0:T(8,128)(2,1)} copy(bf16[128,1024]{0,1:T(8,128)(2,1)S(1)} %bitcast.8) | data formatting | bytes 524288
  (1 shorter events, 0.0 us)
Async XLA Ops:
  3.3 34.9 %all-to-all-start = ((bf16[8,3,128,128]{3,2,1,0:T(8,128)(2,1)}), bf16[8,3,128,128]{3,2,1,0:T(8,128)(2,1)S(1)}, u32[]{:S(2)}, u32[]{:S(2)}) async-start(bf16[8,3,128,128]{3,2,1,0:T(8,128)(2,1)} %bitcast.2), calls=%async_computation | async-start | bytes 1572864 | tf_op jit(solution)/shard_map/all_to_all | solution.py:209
  10.4 38.0 %copy-start.4 = (f32[128]{0:T(128)S(1)}, f32[128]{0:T(128)}, u32[]{:S(2)}) copy-start(f32[128]{0:T(128)} %param.9) | copy-start | bytes 1540
  10.4 38.0 %copy-start.2 = (f32[128,128]{1,0:T(8,128)S(1)}, f32[128,128]{1,0:T(8,128)}, u32[]{:S(2)}) copy-start(f32[128,128]{1,0:T(8,128)} %param.8) | copy-start | bytes 196612
  10.4 19.8 %collective-permute-start = (bf16[3,8,2048]{2,1,0:T(8,128)(2,1)S(1)}, bf16[3,8,2048]{2,1,0:T(8,128)(2,1)S(1)}, u32[]{:S(2)}, u32[]{:S(2)}) collective-permute-start(bf16[3,8,2048]{2,1,0:T(8,128)(2,1)S(1)} %slice.9), channel_id=1, source_target_pairs={{0,2},{2,4},{4,6},{6,8},{8,10},{10,12},{12,14},{1,3},{3,5},{5,7},{... | collective-permute-start | bytes 294920 | tf_op jit(solution)/shard_map/ppermute | solution.py:19
  30.2 0.6 copy-start.1
  36.3 20.6 %collective-permute-start.1 = (bf16[128,2048]{1,0:T(8,128)(2,1)}, bf16[128,2048]{1,0:T(8,128)(2,1)S(1)}, u32[]{:S(2)}, u32[]{:S(2)}) collective-permute-start(bf16[128,2048]{1,0:T(8,128)(2,1)} %get-tuple-element.4.mixed_ref), channel_id=1, source_target_pairs={{0,2},{2,4},{4,6},{6,8},{8,10},{10,12},{12,14},{1,3},{3,5},{5,7},{... | collective-permute-start | bytes 1572872 | tf_op jit(solution)/shard_map/ppermute | solution.py:19
  38.3 0.9 %copy-start = (bf16[8,3,128,128]{3,2,1,0:T(8,128)(2,1)}, bf16[8,3,128,128]{3,2,1,0:T(8,128)(2,1)S(1)}, u32[]{:S(2)}) copy-start(bf16[8,3,128,128]{3,2,1,0:T(8,128)(2,1)S(1)} %all-to-all-done.in_ref) | copy-start | bytes 2359300
  42.7 20.3 %all-to-all-start.1 = ((bf16[8,128,128]{2,1,0:T(8,128)(2,1)}), bf16[8,128,128]{2,1,0:T(8,128)(2,1)S(1)}, u32[]{:S(2)}, u32[]{:S(2)}) async-start(bf16[8,128,128]{2,1,0:T(8,128)(2,1)} %head_attention.1), calls=%async_computation.1 | async-start | bytes 524288 | tf_op jit(solution)/shard_map/all_to_all | solution.py:211
  56.9 0.8 %copy-start.3 = (bf16[128,2048]{1,0:T(8,128)(2,1)}, bf16[128,2048]{1,0:T(8,128)(2,1)S(1)}, u32[]{:S(2)}) copy-start(bf16[128,2048]{1,0:T(8,128)(2,1)S(1)} %collective-permute-done.1.prev_ref) | copy-start | bytes 1572868

commit v2 on v1

--- a/solution.py
+++ b/solution.py
@@ -19,65 +19,171 @@
     return lax.ppermute(block, axis, route)
 
 
-def short_mix(x, edge, short_filter):
+def in_vmem(array):
+    return pltpu.with_memory_space_constraint(array, pltpu.VMEM)
+
+
+ANYWHERE = pl.BlockSpec(memory_space=pl.ANY)
+
+
+def moved(copies):
+    for copy in copies:
+        copy.start()
+    for copy in copies:
+        copy.wait()
+
+
+def by_head(qkv, parts):
+    streams, rows, full = qkv.shape
+    width = full // parts
+
+    def body(qkv_ref, out_ref, sems):
+        moved(
+            [
+                pltpu.make_async_copy(
+                    qkv_ref.at[:, :, pl.ds(p * width, width)], out_ref.at[p], sems.at[p]
+                )
+                for p in range(parts)
+            ]
+        )
+
+    return pl.pallas_call(
+        body,
+        name="by_head",
+        in_specs=[ANYWHERE],
+        out_specs=pl.BlockSpec(memory_space=pltpu.VMEM),
+        out_shape=pltpu.VMEM((parts, streams, rows, width), qkv.dtype),
+        scratch_shapes=[pltpu.SemaphoreType.DMA((parts,))],
+    )(qkv)
+
+
+def by_token(blocks):
+    parts, rows, width = blocks.shape
+
+    def body(in_ref, out_ref, sems):
+        moved(
+            [
+                pltpu.make_async_copy(
+                    in_ref.at[p], out_ref.at[:, pl.ds(p * width, width)], sems.at[p]
+                )
+                for p in range(parts)
+            ]
+        )
+
+    return pl.pallas_call(
+        body,
+        name="by_token",
+        in_specs=[pl.BlockSpec(memory_space=pltpu.VMEM)],
+        out_specs=ANYWHERE,
+        out_shape=jax.ShapeDtypeStruct((rows, parts * width), blocks.dtype),
+        scratch_shapes=[pltpu.SemaphoreType.DMA((parts,))],
+    )(in_vmem(blocks))
+
+
+def tap_sum(filt_ref, s, at, ext, rows):
+    accum = None
+    for j in reversed(range(filt_ref.shape[1])):
+        part = filt_ref[s, j : j + 1, at] * ext[s, pl.ds(EDGE - j, rows), at]
+        accum = part if accum is None else accum + part
+    return accum.astype(jnp.bfloat16)
+
+
+def gated(first, last):
+    return (first.astype(jnp.float32) * last.astype(jnp.float32)).astype(jnp.bfloat16)
+
+
+def short_mix(x, short_filter):
     streams, rows, width = x.shape
-    taps = short_filter.shape[1]
     cols = min(512, width)
 
-    def body(x_ref, edge_ref, filt_ref, mixed_ref, gate_ref, ext_ref):
-        out = []
+    def body(x_ref, filt_ref, parcel_ref, gate_ref, ext_ref):
         for s in range(streams):
-            ext_ref[s, :EDGE, :] = edge_ref[s].astype(jnp.float32)
+            ext_ref[s, :EDGE, :] = jnp.zeros((EDGE, cols), jnp.float32)
             ext_ref[s, EDGE:, :] = x_ref[s].astype(jnp.float32)
         for c in range(cols // LANES):
             at = pl.ds(c * LANES, LANES)
-            out = []
-            for s in range(streams):
-                accum = None
-                for j in reversed(range(taps)):
-                    part = filt_ref[s, j : j + 1, at] * ext_ref[s, pl.ds(EDGE - j, rows), at]
-                    accum = part if accum is None else accum + part
-                out.append(accum.astype(jnp.bfloat16))
-            mixed_ref[:, at] = (out[0].astype(jnp.float32) * out[2].astype(jnp.float32)).astype(
-                jnp.bfloat16
-            )
+            out = [tap_sum(filt_ref, s, at, ext_ref, rows) for s in range(streams)]
+            parcel_ref[:rows, at] = gated(out[0], out[2])
             gate_ref[:, at] = out[1]
-
+        parcel_ref[:EDGE, :] = x_ref[0, :EDGE, :]
+        parcel_ref[rows : rows + EDGE, :] = x_ref[2, :EDGE, :]
+        for s in range(streams):
+            low = rows + (1 + s) * EDGE
+            parcel_ref[low : low + EDGE, :] = x_ref[s, rows - EDGE :, :]
+
+    more = rows + (1 + streams) * EDGE
     return pl.pallas_call(
         body,
         name="short_mix",
         grid=(width // cols,),
         in_specs=[
             pl.BlockSpec((streams, rows, cols), lambda c: (0, 0, c)),
-            pl.BlockSpec((streams, EDGE, cols), lambda c: (0, 0, c)),
-            pl.BlockSpec((streams, taps, cols), lambda c: (0, 0, c)),
+            pl.BlockSpec((streams, short_filter.shape[1], cols), lambda c: (0, 0, c)),
         ],
         out_specs=[
+            pl.BlockSpec((more, cols), lambda c: (0, c)),
             pl.BlockSpec((rows, cols), lambda c: (0, c)),
-            pl.BlockSpec((rows, cols), lambda c: (0, c)),
-        ],
-        out_shape=[jax.ShapeDtypeStruct((rows, width), jnp.bfloat16)] * 2,
+        ],
+        out_shape=[
+            jax.ShapeDtypeStruct((more, width), jnp.bfloat16),
+            jax.ShapeDtypeStruct((rows, width), jnp.bfloat16),
+        ],
         scratch_shapes=[pltpu.VMEM((streams, rows + EDGE, cols), jnp.float32)],
         cost_estimate=pl.CostEstimate(
-            flops=2 * streams * taps * rows * width,
+            flops=2 * streams * short_filter.shape[1] * rows * width,
             transcendentals=0,
             bytes_accessed=10 * rows * width,
         ),
-    )(x, edge, short_filter)
-
-
-def long_conv(prev, mixed, gate, filters_back, skip):
-    rows, width = mixed.shape
+    )(x, short_filter)
+
+
+def long_conv(before, parcel, own, x, gate, short_filter, filters_back, skip):
+    streams, rows, width = x.shape
     taps = filters_back.shape[1]
     cols = min(512, width)
     per_block = LANES // GW
-
-    def body(prev_ref, mixed_ref, gate_ref, filt_ref, skip_ref, out_ref, band_ref):
+    more = own.shape[0]
+
+    def body(
+        before_ref,
+        parcel_ref,
+        own_ref,
+        x_ref,
+        gate_ref,
+        short_ref,
+        filt_ref,
+        skip_ref,
+        out_ref,
+        band_ref,
+        ext_ref,
+        both_ref,
+    ):
         row = lax.broadcasted_iota(jnp.int32, (rows, taps), 0)
         col = lax.broadcasted_iota(jnp.int32, (rows, taps), 1)
         lane_group = lax.broadcasted_iota(jnp.int32, (rows, LANES), 1) // GW
+        starts = {0: 0, 2: rows}
+        for s in range(streams):
+            low = rows + (1 + s) * EDGE
+            ext_ref[s, :EDGE, :] = parcel_ref[low : low + EDGE, :].astype(jnp.float32)
+            ext_ref[s, EDGE:, :] = x_ref[s].astype(jnp.float32)
+        for k, s in enumerate(starts):
+            low = starts[s]
+            ext_ref[streams + s, :EDGE, :] = before_ref[k].astype(jnp.float32)
+            ext_ref[streams + s, EDGE:, :] = parcel_ref[low : low + EDGE, :].astype(jnp.float32)
+        both_ref[:rows, :] = parcel_ref[:rows, :]
+        both_ref[rows:, :] = own_ref[:rows, :]
         for c in range(cols // LANES):
             at = pl.ds(c * LANES, LANES)
+            head = []
+            for base in (0, streams):
+                ends = [
+                    tap_sum(short_ref, s, at, ext_ref.at[pl.ds(base, streams)], EDGE)
+                    for s in starts
+                ]
+                head.append(gated(*ends))
+            both_ref[:EDGE, at] = head[1]
+            both_ref[rows : rows + EDGE, at] = head[0]
+            gate_head = tap_sum(short_ref, 1, at, ext_ref, EDGE)
             for g in range(per_block):
                 base = jnp.broadcast_to(filt_ref[pl.ds(c * per_block + g, 1), :], (rows, taps))
                 ring = pltpu.roll(base, 0, 1, stride=1, stride_axis=0)
@@ -87,38 +193,42 @@
                 band_ref[c, pl.ds(g * rows, rows), taps:] = jnp.where(col <= row, ring, 0.0).astype(
                     jnp.bfloat16
                 )
-            here = mixed_ref[:, at]
-            both = jnp.concatenate([prev_ref[:, at], here], 0)
-            conv_all = jnp.dot(band_ref[c], both, preferred_element_type=jnp.float32)
+            conv_all = jnp.dot(band_ref[c], both_ref[:, at], preferred_element_type=jnp.float32)
             conv = conv_all[:rows]
             for g in range(1, per_block):
                 conv = jnp.where(lane_group == g, conv_all[g * rows : (g + 1) * rows], conv)
-            out_ref[:, at] = (
-                gate_ref[:, at].astype(jnp.float32)
-                * (conv + skip_ref[:, at] * here.astype(jnp.float32))
-            ).astype(jnp.bfloat16)
-
-    wide = pl.BlockSpec((rows, cols), lambda c: (0, c))
+            here = both_ref[rows:, at].astype(jnp.float32)
+            inner = conv + skip_ref[:, at] * here
+            out_ref[:, at] = (gate_ref[:, at].astype(jnp.float32) * inner).astype(jnp.bfloat16)
+            out_ref[:EDGE, at] = (gate_head.astype(jnp.float32) * inner[:EDGE]).astype(jnp.bfloat16)
+
     return pl.pallas_call(
         body,
         name="long_conv",
         grid=(width // cols,),
         in_specs=[
-            wide,
-            wide,
-            wide,
+            pl.BlockSpec((2, EDGE, cols), lambda c: (0, 0, c)),
+            pl.BlockSpec((more, cols), lambda c: (0, c)),
+            pl.BlockSpec((more, cols), lambda c: (0, c)),
+            pl.BlockSpec((streams, EDGE, cols), lambda c: (0, 0, c)),
+            pl.BlockSpec((rows, cols), lambda c: (0, c)),
+            pl.BlockSpec((streams, short_filter.shape[1], cols), lambda c: (0, 0, c)),
             pl.BlockSpec((cols // GW, taps), lambda c: (c, 0)),
             pl.BlockSpec((1, cols), lambda c: (0, c)),
         ],
-        out_specs=wide,
+        out_specs=pl.BlockSpec((rows, cols), lambda c: (0, c)),
         out_shape=jax.ShapeDtypeStruct((rows, width), jnp.bfloat16),
-        scratch_shapes=[pltpu.VMEM((cols // LANES, per_block * rows, 2 * taps), jnp.bfloat16)],
+        scratch_shapes=[
+            pltpu.VMEM((cols // LANES, per_block * rows, 2 * taps), jnp.bfloat16),
+            pltpu.VMEM((2 * streams, 2 * EDGE, cols), jnp.float32),
+            pltpu.VMEM((2 * rows, cols), jnp.bfloat16),
+        ],
         cost_estimate=pl.CostEstimate(
             flops=2 * (width // GW) * LANES * rows * 2 * taps,
             transcendentals=0,
             bytes_accessed=10 * rows * width,
         ),
-    )(prev, mixed, gate, filters_back, skip)
+    )(before, parcel, own, x, gate, short_filter, filters_back, skip)
 
 
 def head_attention(blocks, scale):
@@ -160,13 +270,15 @@
     return pl.pallas_call(
         body,
         name="head_attention",
+        in_specs=[pl.BlockSpec(memory_space=pltpu.VMEM)],
+        out_specs=pl.BlockSpec(memory_space=pltpu.VMEM),
         out_shape=jax.ShapeDtypeStruct((parts, rows, width), jnp.bfloat16),
         cost_estimate=pl.CostEstimate(
             flops=2 * tokens * tokens * width,
             transcendentals=tokens * tokens * width // (2 * HEAD),
             bytes_accessed=8 * tokens * width,
         ),
-    )(blocks)
+    )(in_vmem(blocks))
 
 
 def gathered_attention(qkv, scale):
@@ -201,32 +313,31 @@
     return jnp.concatenate(out_list, 1)
 
 
-def traded_attention(qkv, scale):
+def traded_attention(qkv, scale, early):
     parts = lax.axis_size("ctx")
-    tok_rows = qkv.shape[1]
-    width = qkv.shape[2] // parts
-    outgoing = qkv.reshape(3, tok_rows, parts, width).transpose(2, 0, 1, 3)
-    blocks = lax.all_to_all(outgoing, "ctx", 0, 0, tiled=True)
+    blocks = lax.all_to_all(in_vmem(by_head(qkv, parts)), "ctx", 0, 0, tiled=True)
+    blocks, early = lax.optimization_barrier((blocks, early))
     done = head_attention(blocks, scale)
-    back = lax.all_to_all(done, "ctx", 0, 0, tiled=True)
-    return back.transpose(1, 0, 2).reshape(tok_rows, parts * width)
+    return by_token(lax.all_to_all(done, "ctx", 0, 0, tiled=True)), early
 
 
 def shards(hyena_in, short_filter, mr_taps, mr_decay, skip, qkv):
     tok_rows = hyena_in.shape[1]
     tap_count = mr_taps.shape[1]
     scale = 1.0 / math.sqrt(HEAD)
-    if (qkv.shape[2] // HEAD) % lax.axis_size("ctx") == 0:
-        attn_out = traded_attention(qkv, scale)
-    else:
-        attn_out = gathered_attention(qkv, scale)
-    edge = passed_along(hyena_in[:, tok_rows - EDGE :, :], "ctx", 1)
-    mixed, gate = short_mix(hyena_in, edge, short_filter)
-    prev = passed_along(mixed, "ctx", 1)
+    before = passed_along(hyena_in[::2, tok_rows - EDGE :, :], "ctx", 2)
+    own, gate = short_mix(hyena_in, short_filter)
+    parcel = passed_along(own, "ctx", 1)
     tap_pos = jnp.arange(tap_count, dtype=jnp.float32)
     filters = mr_taps * jnp.exp(-mr_decay[:, None] * tap_pos[None, :])
     filters_back = jnp.concatenate([filters[:, :1], filters[:, :0:-1]], 1)
-    hyena_out = long_conv(prev, mixed, gate, filters_back, skip[None, :])
+    if (qkv.shape[2] // HEAD) % lax.axis_size("ctx") == 0:
+        attn_out, (before, filters_back) = traded_attention(qkv, scale, (before, filters_back))
+    else:
+        attn_out = gathered_attention(qkv, scale)
+    hyena_out = long_conv(
+        before, parcel, own, hyena_in, gate, short_filter, filters_back, skip[None, :]
+    )
     return (hyena_out, attn_out)
 
 

time: 64.7 us -> 54.4 us (0.84)
  the two profiles are of different devices: /device:TPU:16 before, /device:TPU:19 now
where the time goes in v2:
time: 54.4 us; the launch traced here: 53.8 us
  starting transfers between devices  17.1 us (31%)
  Pallas kernels  16.8 us (31%)
  waiting for transfers between devices  16.6 us (31%)
  local copies, waits for them, and re-layouts  1.86 us (3%)
  other arithmetic  0.82 us (2%)
  between operations  0.71 us (1%)
    ppermute x2, waiting for transfers between devices, passed_along(): return lax.ppermute(block, axis, route)  16.6 us
    ppermute x2, starting transfers between devices, passed_along(): return lax.ppermute(block, axis, route)  6.16 us
    pallas_call x1, Pallas kernels, long_conv(): pl.pallas_call(body, name='long_conv', grid=(width // cols,), in_specs=[p...  5.93 us
    all_to_all x1, starting transfers between devices, traded_attention(): lax.all_to_all(in_vmem(by_head(qkv, parts)), 'ctx', 0, 0, tiled=True)  5.75 us
    pallas_call x1, Pallas kernels, short_mix(): pl.pallas_call(body, name='short_mix', grid=(width // cols,), in_specs=[p...  5.44 us
    all_to_all x1, starting transfers between devices, traded_attention(): return (by_token(lax.all_to_all(done, 'ctx', 0, 0, tiled=True)), early)  5.19 us
    pallas_call x1, Pallas kernels, head_attention(): pl.pallas_call(body, name='head_attention', in_specs=[pl.BlockSpec(memory...  2.44 us
    pallas_call x1, Pallas kernels, by_head(): pl.pallas_call(body, name='by_head', in_specs=[ANYWHERE], out_specs=pl.Bl...  2.18 us
  transfers between devices with their start and end apart: 4, of which 2 were waited for; matrix products, arithmetic and copies ran while one was open for 3% of the time, Pallas kernels for 26%

profile of v2, /device:TPU:19, one launch (start us, length us, event | category | flops | bytes accessed | tf_op | source)
XLA Modules:
  0.0 53.8 jit_solution(7085636155772426901)
XLA Ops:
  0.6 2.2 %by_head.1 = bf16[8,3,128,128]{3,2,1,0:T(8,128)(2,1)} custom-call(bf16[3,128,1024]{2,1,0:T(8,128)(2,1)} %qkv_ref.1), custom_call_target="tpu_custom_call" | custom-call | tf_op jit(solution)/shard_map/by_head/pallas_call | solution.py:50
  2.8 0.0 copy-start.3
  2.8 0.0 copy-start.2
  2.8 5.8 %all-to-all-start = ((bf16[8,3,128,128]{3,2,1,0:T(8,128)(2,1)}), bf16[8,3,128,128]{3,2,1,0:T(8,128)(2,1)S(1)}, u32[]{:S(2)}, u32[]{:S(2)}) async-start(bf16[8,3,128,128]{3,2,1,0:T(8,128)(2,1)} %by_head.1), calls=%async_computation | async-start | bytes 1572864 | tf_op jit(solution)/shard_map/all_to_all | solution.py:318
  8.6 0.8 %slice.9 = bf16[2,8,2048]{2,1,0:T(8,128)(2,1)S(1)} slice(bf16[3,128,2048]{2,1,0:T(8,128)(2,1)} %x_ref.3), slice={[0:3:2], [120:128:1], [0:2048:1]} | slice | bytes 131072 | tf_op jit(solution)/shard_map/slice | solution.py:328
  9.4 3.1 %collective-permute-start = (bf16[2,8,2048]{2,1,0:T(8,128)(2,1)S(1)}, bf16[2,8,2048]{2,1,0:T(8,128)(2,1)S(1)}, u32[]{:S(2)}, u32[]{:S(2)}) collective-permute-start(bf16[2,8,2048]{2,1,0:T(8,128)(2,1)S(1)} %slice.9), channel_id=1, source_target_pairs={{0,4},{2,6},{4,8},{6,10},{8,12},{10,14},{1,5},{3,7},{5,9},{7,11},{... | collective-permute-start | bytes 196616 | tf_op jit(solution)/shard_map/ppermute | solution.py:19
  12.5 5.4 %short_mix.1 = (bf16[160,2048]{1,0:T(8,128)(2,1)}, bf16[128,2048]{1,0:T(8,128)(2,1)}) custom-call(bf16[3,128,2048]{2,1,0:T(8,128)(2,1)} %x_ref.3, f32[3,7,2048]{2,1,0:T(8,128)} %short_ref.1), custom_call_target="tpu_custom_call" | custom-call | flops 11010048 | bytes 2621440 | tf_op jit(solution)/shard_map/short_mix/pallas_call | solution.py:115
  18.0 3.1 %collective-permute-start.1 = (bf16[160,2048]{1,0:T(8,128)(2,1)}, bf16[160,2048]{1,0:T(8,128)(2,1)S(1)}, u32[]{:S(2)}, u32[]{:S(2)}) collective-permute-start(bf16[160,2048]{1,0:T(8,128)(2,1)} %get-tuple-element.8.own_ref), channel_id=1, source_target_pairs={{0,2},{2,4},{4,6},{6,8},{8,10},{10,12},{12,14},{1,3},{3,5},{5,7},{... | collective-permute-start | bytes 1966088 | tf_op jit(solution)/shard_map/ppermute | solution.py:19
  21.0 0.0 copy-done.3
  21.1 0.0 copy-done.2
  21.1 0.1 exponential_multiply_fusion
  21.2 0.1 slice.13
  21.3 0.1 rev.3
  21.3 0.7 %pad_maximum_fusion.filt_ref = f32[128,128]{1,0:T(8,128)} fusion(f32[128,127]{1,0:T(8,128)S(1)} %rev.3, f32[128,1]{1,0:T(8,128)S(1)} %bitcast.2), kind=kLoop, calls=%fused_computation | loop fusion | flops 16384 | bytes 131072 | tf_op jit(solution)/shard_map/concatenate | solution.py:333
  22.1 5.8 %collective-permute-done.before_ref = bf16[2,8,2048]{2,1,0:T(8,128)(2,1)S(1)} collective-permute-done((bf16[2,8,2048]{2,1,0:T(8,128)(2,1)S(1)}, bf16[2,8,2048]{2,1,0:T(8,128)(2,1)S(1)}, u32[]{:S(2)}, u32[]{:S(2)}) %collective-permute-start) | collective-permute-done | bytes 65568 | tf_op jit(solution)/shard_map/ppermute | solution.py:19
  27.9 0.0 copy-start.1
  27.9 0.0 all-to-all-done.in_ref
  27.9 2.4 %head_attention.1 = bf16[8,128,128]{2,1,0:T(8,128)(2,1)} custom-call(bf16[8,3,128,128]{3,2,1,0:T(8,128)(2,1)S(1)} %all-to-all-done.in_ref), custom_call_target="tpu_custom_call" | custom-call | flops 268435456 | bytes 1048576 | tf_op jit(solution)/shard_map/head_attention/pallas_call | solution.py:270
  30.3 5.2 %all-to-all-start.1 = ((bf16[8,128,128]{2,1,0:T(8,128)(2,1)}), bf16[8,128,128]{2,1,0:T(8,128)(2,1)S(1)}, u32[]{:S(2)}, u32[]{:S(2)}) async-start(bf16[8,128,128]{2,1,0:T(8,128)(2,1)} %head_attention.1), calls=%async_computation.1 | async-start | bytes 524288 | tf_op jit(solution)/shard_map/all_to_all | solution.py:321
  35.5 10.8 %collective-permute-done.1.parcel_ref = bf16[160,2048]{1,0:T(8,128)(2,1)S(1)} collective-permute-done((bf16[160,2048]{1,0:T(8,128)(2,1)}, bf16[160,2048]{1,0:T(8,128)(2,1)S(1)}, u32[]{:S(2)}, u32[]{:S(2)}) %collective-permute-start.1) | collective-permute-done | bytes 655392 | tf_op jit(solution)/shard_map/ppermute | solution.py:19
  46.3 0.0 copy-start
  46.3 0.0 copy-done.1
  46.3 0.8 %copy-done = bf16[160,2048]{1,0:T(8,128)(2,1)} copy-done((bf16[160,2048]{1,0:T(8,128)(2,1)}, bf16[160,2048]{1,0:T(8,128)(2,1)S(1)}, u32[]{:S(2)}) %copy-start) | copy-done | bytes 655384
  47.1 5.9 %long_conv.1 = bf16[128,2048]{1,0:T(8,128)(2,1)} custom-call(bf16[2,8,2048]{2,1,0:T(8,128)(2,1)} %copy-done.1, bf16[160,2048]{1,0:T(8,128)(2,1)} %copy-done, bf16[160,2048]{1,0:T(8,128)(2,1)} %get-tuple-element.8.own_ref, bf16[3,128,2048]{2,1,0:T(8,128)(2,1)} %x_ref.3, bf16[128,2048]{1,0:T(8,128)(2,1)} %get-tuple-element.9.gate_ref, ...), custom_call_target="tpu_custom_call" | custom-call | flops 1073741824 | bytes 2621440 | tf_op jit(solution)/shard_map/long_conv/pallas_call | solution.py:205
  53.1 0.0 all-to-all-done.1.in_ref
  53.1 0.8 %by_token.1 = bf16[128,1024]{1,0:T(8,128)(2,1)} custom-call(bf16[8,128,128]{2,1,0:T(8,128)(2,1)S(1)} %all-to-all-done.1.in_ref), custom_call_target="tpu_custom_call" | custom-call | tf_op jit(solution)/shard_map/by_token/pallas_call | solution.py:73
  (1 shorter events, 0.0 us)
Async XLA Ops:
  2.8 18.2 %copy-start.3 = (f32[128]{0:T(128)S(1)}, f32[128]{0:T(128)}, u32[]{:S(2)}) copy-start(f32[128]{0:T(128)} %param.9) | copy-start | bytes 1540
  2.8 18.2 %copy-start.2 = (f32[128,128]{1,0:T(8,128)S(1)}, f32[128,128]{1,0:T(8,128)}, u32[]{:S(2)}) copy-start(f32[128,128]{1,0:T(8,128)} %param.8) | copy-start | bytes 196612
  2.8 25.0 %all-to-all-start = ((bf16[8,3,128,128]{3,2,1,0:T(8,128)(2,1)}), bf16[8,3,128,128]{3,2,1,0:T(8,128)(2,1)S(1)}, u32[]{:S(2)}, u32[]{:S(2)}) async-start(bf16[8,3,128,128]{3,2,1,0:T(8,128)(2,1)} %by_head.1), calls=%async_computation | async-start | bytes 1572864 | tf_op jit(solution)/shard_map/all_to_all | solution.py:318
  9.4 18.4 %collective-permute-start = (bf16[2,8,2048]{2,1,0:T(8,128)(2,1)S(1)}, bf16[2,8,2048]{2,1,0:T(8,128)(2,1)S(1)}, u32[]{:S(2)}, u32[]{:S(2)}) collective-permute-start(bf16[2,8,2048]{2,1,0:T(8,128)(2,1)S(1)} %slice.9), channel_id=1, source_target_pairs={{0,4},{2,6},{4,8},{6,10},{8,12},{10,14},{1,5},{3,7},{5,9},{7,11},{... | collective-permute-start | bytes 196616 | tf_op jit(solution)/shard_map/ppermute | solution.py:19
  18.0 28.3 %collective-permute-start.1 = (bf16[160,2048]{1,0:T(8,128)(2,1)}, bf16[160,2048]{1,0:T(8,128)(2,1)S(1)}, u32[]{:S(2)}, u32[]{:S(2)}) collective-permute-start(bf16[160,2048]{1,0:T(8,128)(2,1)} %get-tuple-element.8.own_ref), channel_id=1, source_target_pairs={{0,2},{2,4},{4,6},{6,8},{8,10},{10,12},{12,14},{1,3},{3,5},{5,7},{... | collective-permute-start | bytes 1966088 | tf_op jit(solution)/shard_map/ppermute | solution.py:19
  27.9 18.4 %copy-start.1 = (bf16[2,8,2048]{2,1,0:T(8,128)(2,1)}, bf16[2,8,2048]{2,1,0:T(8,128)(2,1)S(1)}, u32[]{:S(2)}) copy-start(bf16[2,8,2048]{2,1,0:T(8,128)(2,1)S(1)} %collective-permute-done.before_ref) | copy-start | bytes 196612
  30.3 22.7 %all-to-all-start.1 = ((bf16[8,128,128]{2,1,0:T(8,128)(2,1)}), bf16[8,128,128]{2,1,0:T(8,128)(2,1)S(1)}, u32[]{:S(2)}, u32[]{:S(2)}) async-start(bf16[8,128,128]{2,1,0:T(8,128)(2,1)} %head_attention.1), calls=%async_computation.1 | async-start | bytes 524288 | tf_op jit(solution)/shard_map/all_to_all | solution.py:321
  46.3 0.8 %copy-start = (bf16[160,2048]{1,0:T(8,128)(2,1)}, bf16[160,2048]{1,0:T(8,128)(2,1)S(1)}, u32[]{:S(2)}) copy-start(bf16[160,2048]{1,0:T(8,128)(2,1)S(1)} %collective-permute-done.1.parcel_ref) | copy-start | bytes 1966084

commit v3 on v1

v3 whole, which is shorter than its diff:
```python
import math

import jax
import jax.numpy as jnp
from jax import lax
from jax.experimental import pallas as pl
from jax.experimental.pallas import tpu as pltpu
from jax.sharding import PartitionSpec as P

HEAD = 128
GW = 16
LANES = 128
EDGE = 8


def passed_along(block, axis, distance):
    devices = range(lax.axis_size(axis))
    route = [(i - distance, i) for i in devices if i - distance in devices]
    return lax.ppermute(block, axis, route)


def in_vmem(array):
    return pltpu.with_memory_space_constraint(array, pltpu.VMEM)


ANYWHERE = pl.BlockSpec(memory_space=pl.ANY)


def moved(copies):
    for copy in copies:
        copy.start()
    for copy in copies:
        copy.wait()


def by_head(qkv, parts):
    streams, rows, full = qkv.shape
    width = full // parts

    def body(qkv_ref, out_ref):
        for p in range(parts):
            out_ref[p] = qkv_ref[:, :, pl.ds(p * width, width)]

    return pl.pallas_call(
        body,
        name="by_head",
        in_specs=[pl.BlockSpec(memory_space=pltpu.VMEM)],
        out_specs=pl.BlockSpec(memory_space=pltpu.VMEM),
        out_shape=pltpu.VMEM((parts, streams, rows, width), qkv.dtype),
    )(in_vmem(qkv))


def by_token(blocks):
    parts, rows, width = blocks.shape

    def body(in_ref, out_ref, sems):
        moved(
            [
                pltpu.make_async_copy(
                    in_ref.at[p], out_ref.at[:, pl.ds(p * width, width)], sems.at[p]
                )
                for p in range(parts)
            ]
        )

    return pl.pallas_call(
        body,
        name="by_token",
        in_specs=[pl.BlockSpec(memory_space=pltpu.VMEM)],
        out_specs=ANYWHERE,
        out_shape=jax.ShapeDtypeStruct((rows, parts * width), blocks.dtype),
        scratch_shapes=[pltpu.SemaphoreType.DMA((parts,))],
    )(in_vmem(blocks))


def hyena_local(x, edge, short_filter, filters_back, skip):
    streams, rows, width = x.shape
    short_taps = short_filter.shape[1]
    taps = filters_back.shape[1]
    cols = min(512, width)
    per_block = LANES // GW

    def body(x_ref, edge_ref, short_ref, filt_ref, skip_ref, onward_ref, part_ref, gate_ref, *held):
        ext_ref, band_ref, twice_ref = held
        row = lax.broadcasted_iota(jnp.int32, (rows, taps), 0)
        col = lax.broadcasted_iota(jnp.int32, (rows, taps), 1)
        lane_group = (lax.broadcasted_iota(jnp.int32, (rows, 2 * LANES), 1) % LANES) // GW
        twice_ref[:rows, LANES:] = jnp.zeros((rows, LANES), jnp.bfloat16)
        twice_ref[rows:, :LANES] = jnp.zeros((rows, LANES), jnp.bfloat16)
        for s in range(streams):
            ext_ref[s, :EDGE, :] = edge_ref[s].astype(jnp.float32)
            ext_ref[s, EDGE:, :] = x_ref[s].astype(jnp.float32)
        for c in range(cols // LANES):
            at = pl.ds(c * LANES, LANES)
            out = []
            for s in range(streams):
                accum = None
                for j in reversed(range(short_taps)):
                    piece = short_ref[s, j : j + 1, at] * ext_ref[s, pl.ds(EDGE - j, rows), at]
                    accum = piece if accum is None else accum + piece
                out.append(accum.astype(jnp.bfloat16))
            mixed = (out[0].astype(jnp.float32) * out[2].astype(jnp.float32)).astype(jnp.bfloat16)
            gate_ref[:, at] = out[1]
            twice_ref[:rows, :LANES] = mixed
            twice_ref[rows:, LANES:] = mixed
            for g in range(per_block):
                base = jnp.broadcast_to(filt_ref[pl.ds(c * per_block + g, 1), :], (rows, taps))
                ring = pltpu.roll(base, 0, 1, stride=1, stride_axis=0)
                at_g = pl.ds(g * rows, rows)
                band_ref[at_g, :taps] = jnp.where(col > row, ring, 0.0).astype(jnp.bfloat16)
                band_ref[at_g, taps:] = jnp.where(col <= row, ring, 0.0).astype(jnp.bfloat16)
            every = jnp.dot(band_ref[...], twice_ref[...], preferred_element_type=jnp.float32)
            conv = every[:rows]
            for g in range(1, per_block):
                conv = jnp.where(lane_group == g, every[g * rows : (g + 1) * rows], conv)
            onward_ref[:, at] = conv[:, :LANES].astype(jnp.bfloat16)
            part_ref[:, at] = conv[:, LANES:] + skip_ref[:, at] * mixed.astype(jnp.float32)

    wide = pl.BlockSpec((rows, cols), lambda c: (0, c))
    return pl.pallas_call(
        body,
        name="hyena_local",
        grid=(width // cols,),
        in_specs=[
            pl.BlockSpec((streams, rows, cols), lambda c: (0, 0, c)),
            pl.BlockSpec((streams, EDGE, cols), lambda c: (0, 0, c)),
            pl.BlockSpec((streams, short_taps, cols), lambda c: (0, 0, c)),
            pl.BlockSpec((cols // GW, taps), lambda c: (c, 0)),
            pl.BlockSpec((1, cols), lambda c: (0, c)),
        ],
        out_specs=[wide, wide, wide],
        out_shape=[
            jax.ShapeDtypeStruct((rows, width), jnp.bfloat16),
            jax.ShapeDtypeStruct((rows, width), jnp.float32),
            jax.ShapeDtypeStruct((rows, width), jnp.bfloat16),
        ],
        scratch_shapes=[
            pltpu.VMEM((streams, rows + EDGE, cols), jnp.float32),
            pltpu.VMEM((per_block * rows, 2 * taps), jnp.bfloat16),
            pltpu.VMEM((2 * rows, 2 * LANES), jnp.bfloat16),
        ],
        cost_estimate=pl.CostEstimate(
            flops=4 * (width // GW) * LANES * rows * 2 * taps,
            transcendentals=0,
            bytes_accessed=14 * rows * width,
        ),
    )(x, edge, short_filter, filters_back, skip)


def head_attention(blocks, scale):
    parts, _, rows, width = blocks.shape
    step = 2 if parts % 2 == 0 else 1
    q_rows = step * rows

    def body(in_ref, out_ref):
        row = lax.broadcasted_iota(jnp.int32, (q_rows, q_rows), 0)
        col = lax.broadcasted_iota(jnp.int32, (q_rows, q_rows), 1)
        keep = col <= row
        for h in range(width // HEAD):
            at = pl.ds(h * HEAD, HEAD)
            for b in range(parts // step):
                upto = (b + 1) * step
                query = in_ref[b * step : upto, 0, :, at].reshape(q_rows, HEAD)
                keys = in_ref[:upto, 1, :, at].reshape(upto * rows, HEAD)
                values = in_ref[:upto, 2, :, at].reshape(upto * rows, HEAD)
                scores = lax.dot_general(
                    query, keys, (((1,), (1,)), ((), ())), preferred_element_type=jnp.float32
                )
                low = b * q_rows
                edge_scores = jnp.where(keep, scores[:, low:], -1e30)
                if b:
                    scores = jnp.concatenate([scores[:, :low], edge_scores], 1)
                else:
                    scores = edge_scores
                top = jnp.max(scores, axis=1, keepdims=True)
                weights = jnp.exp((scores - top) * scale)
                total = jnp.sum(weights, axis=1, keepdims=True)
                summed = jnp.dot(
                    weights.astype(jnp.bfloat16), values, preferred_element_type=jnp.float32
                )
                out_ref[b * step : upto, :, at] = (
                    (summed / total).astype(jnp.bfloat16).reshape(step, rows, HEAD)
                )

    tokens = parts * rows
    return pl.pallas_call(
        body,
        name="head_attention",
        in_specs=[pl.BlockSpec(memory_space=pltpu.VMEM)],
        out_specs=pl.BlockSpec(memory_space=pltpu.VMEM),
        out_shape=jax.ShapeDtypeStruct((parts, rows, width), jnp.bfloat16),
        cost_estimate=pl.CostEstimate(
            flops=2 * tokens * tokens * width,
            transcendentals=tokens * tokens * width // (2 * HEAD),
            bytes_accessed=8 * tokens * width,
        ),
    )(in_vmem(blocks))


def gathered_attention(qkv, scale):
    tok_rows = qkv.shape[1]
    head_count = qkv.shape[2] // HEAD
    queries = qkv[0]
    query_pos = lax.axis_index("ctx") * tok_rows + jnp.arange(tok_rows, dtype=jnp.int32)
    block_pair = lax.all_gather(qkv[1:3], "ctx", axis=1, tiled=True)
    key_pos = jnp.arange(block_pair.shape[1], dtype=jnp.int32)
    causal_mask = key_pos[None, :] <= query_pos[:, None]
    out_list = []
    for head_index in range(head_count):
        cols = slice(head_index * HEAD, (head_index + 1) * HEAD)
        scores = (
            lax.dot_general(
                queries[:, cols],
                block_pair[0][:, cols],
                (((1,), (1,)), ((), ())),
                preferred_element_type=jnp.float32,
            )
            * scale
        )
        top = jnp.max(jnp.where(causal_mask, scores, -1e30), axis=1)
        weights = jnp.where(causal_mask, jnp.exp(scores - top[:, None]), 0.0)
        total = jnp.sum(weights, axis=1)
        summed = jnp.dot(
            weights.astype(jnp.bfloat16),
            block_pair[1][:, cols],
            preferred_element_type=jnp.float32,
        )
        out_list.append((summed / total[:, None]).astype(jnp.bfloat16))
    return jnp.concatenate(out_list, 1)


def shards(hyena_in, short_filter, mr_taps, mr_decay, skip, qkv):
    tok_rows = hyena_in.shape[1]
    tap_count = mr_taps.shape[1]
    parts = lax.axis_size("ctx")
    scale = 1.0 / math.sqrt(HEAD)
    traded = (qkv.shape[2] // HEAD) % parts == 0
    edge = passed_along(hyena_in[:, tok_rows - EDGE :, :], "ctx", 1)
    if traded:
        outgoing, edge = lax.optimization_barrier((by_head(qkv, parts), edge))
        blocks = lax.all_to_all(outgoing, "ctx", 0, 0, tiled=True)
    tap_pos = jnp.arange(tap_count, dtype=jnp.float32)
    filters = mr_taps * jnp.exp(-mr_decay[:, None] * tap_pos[None, :])
    filters_back = jnp.concatenate([filters[:, :1], filters[:, :0:-1]], 1)
    onward, part, gate = hyena_local(hyena_in, edge, short_filter, filters_back, skip[None, :])
    carried = passed_along(onward, "ctx", 1)
    if traded:
        done = head_attention(blocks, scale)
        attn_out = by_token(lax.all_to_all(done, "ctx", 0, 0, tiled=True))
    else:
        attn_out = gathered_attention(qkv, scale)
    hyena_out = (gate.astype(jnp.float32) * (part + carried.astype(jnp.float32))).astype(
        jnp.bfloat16
    )
    return (hyena_out, attn_out)


def solution(mesh):
    placed = (
        P(None, ("groups", "ctx"), "tp"),
        P(None, None, "tp"),
        P("tp", None),
        P("tp"),
        P("tp"),
        P(None, ("groups", "ctx"), "tp"),
    )
    return jax.shard_map(
        shards,
        mesh=mesh,
        in_specs=placed,
        out_specs=(P(("groups", "ctx"), "tp"), P(("groups", "ctx"), "tp")),
        check_vma=False,
    )
```

time: 64.7 us -> 50.5 us (0.78)
  the two profiles are of different devices: /device:TPU:16 before, /device:TPU:0 now
where the time goes in v3:
time: 50.5 us; the launch traced here: 50.1 us
  starting transfers between devices  19.7 us (39%)
  Pallas kernels  13.4 us (27%)
  waiting for transfers between devices  12.3 us (24%)
  local copies, waits for them, and re-layouts  2.21 us (4%)
  other arithmetic  1.81 us (4%)
  between operations  0.71 us (1%)
    pallas_call x1, Pallas kernels, hyena_local(): pl.pallas_call(body, name='hyena_local', grid=(width // cols,), in_specs=...  9.14 us
    ppermute x2, starting transfers between devices, passed_along(): return lax.ppermute(block, axis, route)  8.94 us
    all_to_all x1, waiting for transfers between devices, shards(): attn_out = by_token(lax.all_to_all(done, 'ctx', 0, 0, tiled=True))  7.37 us
    all_to_all x1, starting transfers between devices, shards(): blocks = lax.all_to_all(outgoing, 'ctx', 0, 0, tiled=True)  6.7 us
    all_to_all x1, waiting for transfers between devices, shards(): blocks = lax.all_to_all(outgoing, 'ctx', 0, 0, tiled=True)  4.89 us
    all_to_all x1, starting transfers between devices, shards(): attn_out = by_token(lax.all_to_all(done, 'ctx', 0, 0, tiled=True))  4.02 us
    pallas_call x1, Pallas kernels, head_attention(): pl.pallas_call(body, name='head_attention', in_specs=[pl.BlockSpec(memory...  2.44 us
    unnamed x12, local copies, waits for them, and re-layouts  1.15 us
  transfers between devices with their start and end apart: 4, of which 2 were waited for; matrix products, arithmetic and copies ran while one was open for 4% of the time, Pallas kernels for 25%

profile of v3, /device:TPU:0, one launch (start us, length us, event | category | flops | bytes accessed | tf_op | source)
XLA Modules:
  0.0 50.1 jit_solution(13477297654659662871)
XLA Ops:
  0.6 0.9 %slice.9 = bf16[3,8,2048]{2,1,0:T(8,128)(2,1)S(1)} slice(bf16[3,128,2048]{2,1,0:T(8,128)(2,1)} %x_ref.1), slice={[0:3], [120:128], [0:2048]} | slice | bytes 196608 | tf_op jit(solution)/shard_map/slice | solution.py:238
  1.5 4.9 %collective-permute-start = (bf16[3,8,2048]{2,1,0:T(8,128)(2,1)S(1)}, bf16[3,8,2048]{2,1,0:T(8,128)(2,1)S(1)}, u32[]{:S(2)}, u32[]{:S(2)}) collective-permute-start(bf16[3,8,2048]{2,1,0:T(8,128)(2,1)S(1)} %slice.9), channel_id=1, source_target_pairs={{0,2},{2,4},{4,6},{6,8},{8,10},{10,12},{12,14},{1,3},{3,5},{5,7},{... | collective-permute-start | bytes 294920 | tf_op jit(solution)/shard_map/ppermute | solution.py:19
  6.4 0.0 copy-start
  6.4 1.1 %copy-done = bf16[3,128,1024]{2,1,0:T(8,128)(2,1)S(1)} copy-done((bf16[3,128,1024]{2,1,0:T(8,128)(2,1)S(1)}, bf16[3,128,1024]{2,1,0:T(8,128)(2,1)}, u32[]{:S(2)}) %copy-start) | copy-done | bytes 786456
  7.5 0.0 copy-start.5
  7.5 0.0 copy-start.3
  7.5 1.1 %by_head.1 = bf16[8,3,128,128]{3,2,1,0:T(8,128)(2,1)} custom-call(bf16[3,128,1024]{2,1,0:T(8,128)(2,1)S(1)} %copy-done), custom_call_target="tpu_custom_call" | custom-call | tf_op jit(solution)/shard_map/by_head/pallas_call | solution.py:44
  8.6 0.0 collective-permute-done.edge_ref
  8.6 0.0 copy-start.4
  8.6 6.7 %all-to-all-start = ((bf16[8,3,128,128]{3,2,1,0:T(8,128)(2,1)}), bf16[8,3,128,128]{3,2,1,0:T(8,128)(2,1)S(1)}, u32[]{:S(2)}, u32[]{:S(2)}) async-start(bf16[8,3,128,128]{3,2,1,0:T(8,128)(2,1)} %by_head.1), calls=%async_computation | async-start | bytes 1572864 | tf_op jit(solution)/shard_map/all_to_all | solution.py:241
  15.3 0.0 copy-done.5
  15.3 0.0 copy-done.3
  15.3 0.1 exponential_multiply_fusion
  15.4 0.1 slice.13
  15.5 0.1 rev.3
  15.6 0.7 %pad_maximum_fusion.filt_ref = f32[128,128]{1,0:T(8,128)} fusion(f32[128,127]{1,0:T(8,128)S(1)} %rev.3, f32[128,1]{1,0:T(8,128)S(1)} %bitcast.2), kind=kLoop, calls=%fused_computation.1 | loop fusion | flops 16384 | bytes 131072 | tf_op jit(solution)/shard_map/concatenate | solution.py:244
  16.3 0.0 copy-done.4
  16.3 9.1 %hyena_local.1 = (bf16[128,2048]{1,0:T(8,128)(2,1)}, f32[128,2048]{1,0:T(8,128)}, bf16[128,2048]{1,0:T(8,128)(2,1)}) custom-call(bf16[3,128,2048]{2,1,0:T(8,128)(2,1)} %x_ref.1, bf16[3,8,2048]{2,1,0:T(8,128)(2,1)} %copy-done.4, f32[3,7,2048]{2,1,0:T(8,128)} %short_ref.1, f32[128,128]{1,0:T(8,128)} %pad_maximum_fusion.filt_ref, f32[1,2048]{1,0:T(1,128)} %bitcast.3), custom_call_target="tpu_custom_call" | custom-call | flops 2147483648 | bytes 3670016 | tf_op jit(solution)/shard_map/hyena_local/pallas_call | solution.py:120
  25.5 0.0 copy-start.1
  25.5 0.0 copy-start.2
  25.5 4.1 %collective-permute-start.1 = (bf16[128,2048]{1,0:T(8,128)(2,1)}, bf16[128,2048]{1,0:T(8,128)(2,1)S(1)}, u32[]{:S(2)}, u32[]{:S(2)}) collective-permute-start(bf16[128,2048]{1,0:T(8,128)(2,1)} %get-tuple-element.10), channel_id=1, source_target_pairs={{0,2},{2,4},{4,6},{6,8},{8,10},{10,12},{12,14},{1,3},{3,5},{5,7},{... | collective-permute-start | bytes 1572872 | tf_op jit(solution)/shard_map/ppermute | solution.py:19
  29.6 4.9 %all-to-all-done.in_ref = bf16[8,3,128,128]{3,2,1,0:T(8,128)(2,1)S(1)} async-done(((bf16[8,3,128,128]{3,2,1,0:T(8,128)(2,1)}), bf16[8,3,128,128]{3,2,1,0:T(8,128)(2,1)S(1)}, u32[]{:S(2)}, u32[]{:S(2)}) %all-to-all-start) | async-done | bytes 786464 | tf_op jit(solution)/shard_map/all_to_all | solution.py:241
  34.5 2.4 %head_attention.1 = bf16[8,128,128]{2,1,0:T(8,128)(2,1)} custom-call(bf16[8,3,128,128]{3,2,1,0:T(8,128)(2,1)S(1)} %all-to-all-done.in_ref), custom_call_target="tpu_custom_call" | custom-call | flops 268435456 | bytes 1048576 | tf_op jit(solution)/shard_map/head_attention/pallas_call | solution.py:186
  36.9 4.0 %all-to-all-start.1 = ((bf16[8,128,128]{2,1,0:T(8,128)(2,1)}), bf16[8,128,128]{2,1,0:T(8,128)(2,1)S(1)}, u32[]{:S(2)}, u32[]{:S(2)}) async-start(bf16[8,128,128]{2,1,0:T(8,128)(2,1)} %head_attention.1), calls=%async_computation.1 | async-start | bytes 524288 | tf_op jit(solution)/shard_map/all_to_all | solution.py:249
  40.9 0.0 collective-permute-done.1
  40.9 0.0 copy-done.1
  40.9 0.0 copy-done.2
  40.9 1.0 %multiply_convert_fusion = bf16[128,2048]{1,0:T(8,128)(2,1)} fusion(f32[128,2048]{1,0:T(8,128)S(1)} %copy-done.1, bf16[128,2048]{1,0:T(8,128)(2,1)S(1)} %collective-permute-done.1, bf16[128,2048]{1,0:T(8,128)(2,1)S(1)} %copy-done.2), kind=kLoop, calls=%fused_computation | loop fusion | flops 1310720 | bytes 2621440 | tf_op jit(solution)/shard_map/convert_element_type | solution.py:252
  41.9 7.4 %all-to-all-done.1.in_ref = bf16[8,128,128]{2,1,0:T(8,128)(2,1)S(1)} async-done(((bf16[8,128,128]{2,1,0:T(8,128)(2,1)}), bf16[8,128,128]{2,1,0:T(8,128)(2,1)S(1)}, u32[]{:S(2)}, u32[]{:S(2)}) %all-to-all-start.1) | async-done | bytes 262176 | tf_op jit(solution)/shard_map/all_to_all | solution.py:249
  49.3 0.8 %by_token.1 = bf16[128,1024]{1,0:T(8,128)(2,1)} custom-call(bf16[8,128,128]{2,1,0:T(8,128)(2,1)S(1)} %all-to-all-done.1.in_ref), custom_call_target="tpu_custom_call" | custom-call | tf_op jit(solution)/shard_map/by_token/pallas_call | solution.py:66
  (1 shorter events, 0.0 us)
Async XLA Ops:
  1.5 7.1 %collective-permute-start = (bf16[3,8,2048]{2,1,0:T(8,128)(2,1)S(1)}, bf16[3,8,2048]{2,1,0:T(8,128)(2,1)S(1)}, u32[]{:S(2)}, u32[]{:S(2)}) collective-permute-start(bf16[3,8,2048]{2,1,0:T(8,128)(2,1)S(1)} %slice.9), channel_id=1, source_target_pairs={{0,2},{2,4},{4,6},{6,8},{8,10},{10,12},{12,14},{1,3},{3,5},{5,7},{... | collective-permute-start | bytes 294920 | tf_op jit(solution)/shard_map/ppermute | solution.py:19
  6.4 1.1 %copy-start = (bf16[3,128,1024]{2,1,0:T(8,128)(2,1)S(1)}, bf16[3,128,1024]{2,1,0:T(8,128)(2,1)}, u32[]{:S(2)}) copy-start(bf16[3,128,1024]{2,1,0:T(8,128)(2,1)} %qkv_ref.1) | copy-start | bytes 2359300
  7.5 7.8 %copy-start.5 = (f32[128]{0:T(128)S(1)}, f32[128]{0:T(128)}, u32[]{:S(2)}) copy-start(f32[128]{0:T(128)} %param.9) | copy-start | bytes 1540
  7.5 7.8 %copy-start.3 = (f32[128,128]{1,0:T(8,128)S(1)}, f32[128,128]{1,0:T(8,128)}, u32[]{:S(2)}) copy-start(f32[128,128]{1,0:T(8,128)} %param.8) | copy-start | bytes 196612
  8.6 7.7 %copy-start.4 = (bf16[3,8,2048]{2,1,0:T(8,128)(2,1)}, bf16[3,8,2048]{2,1,0:T(8,128)(2,1)S(1)}, u32[]{:S(2)}) copy-start(bf16[3,8,2048]{2,1,0:T(8,128)(2,1)S(1)} %collective-permute-done.edge_ref) | copy-start | bytes 294916
  8.6 25.8 %all-to-all-start = ((bf16[8,3,128,128]{3,2,1,0:T(8,128)(2,1)}), bf16[8,3,128,128]{3,2,1,0:T(8,128)(2,1)S(1)}, u32[]{:S(2)}, u32[]{:S(2)}) async-start(bf16[8,3,128,128]{3,2,1,0:T(8,128)(2,1)} %by_head.1), calls=%async_computation | async-start | bytes 1572864 | tf_op jit(solution)/shard_map/all_to_all | solution.py:241
  25.5 15.5 %copy-start.1 = (f32[128,2048]{1,0:T(8,128)S(1)}, f32[128,2048]{1,0:T(8,128)}, u32[]{:S(2)}) copy-start(f32[128,2048]{1,0:T(8,128)} %get-tuple-element.9) | copy-start | bytes 3145732
  25.5 15.5 %copy-start.2 = (bf16[128,2048]{1,0:T(8,128)(2,1)S(1)}, bf16[128,2048]{1,0:T(8,128)(2,1)}, u32[]{:S(2)}) copy-start(bf16[128,2048]{1,0:T(8,128)(2,1)} %get-tuple-element.8) | copy-start | bytes 1572868
  25.5 15.4 %collective-permute-start.1 = (bf16[128,2048]{1,0:T(8,128)(2,1)}, bf16[128,2048]{1,0:T(8,128)(2,1)S(1)}, u32[]{:S(2)}, u32[]{:S(2)}) collective-permute-start(bf16[128,2048]{1,0:T(8,128)(2,1)} %get-tuple-element.10), channel_id=1, source_target_pairs={{0,2},{2,4},{4,6},{6,8},{8,10},{10,12},{12,14},{1,3},{3,5},{5,7},{... | collective-permute-start | bytes 1572872 | tf_op jit(solution)/shard_map/ppermute | solution.py:19
  36.9 12.4 %all-to-all-start.1 = ((bf16[8,128,128]{2,1,0:T(8,128)(2,1)}), bf16[8,128,128]{2,1,0:T(8,128)(2,1)S(1)}, u32[]{:S(2)}, u32[]{:S(2)}) async-start(bf16[8,128,128]{2,1,0:T(8,128)(2,1)} %head_attention.1), calls=%async_computation.1 | async-start | bytes 524288 | tf_op jit(solution)/shard_map/all_to_all | solution.py:249

commit v4 on v3

--- a/solution.py
+++ b/solution.py
@@ -11,6 +11,7 @@
 GW = 16
 LANES = 128
 EDGE = 8
+REACH = 16
 
 
 def passed_along(block, axis, distance):
@@ -48,6 +49,35 @@
         out_specs=pl.BlockSpec(memory_space=pltpu.VMEM),
         out_shape=pltpu.VMEM((parts, streams, rows, width), qkv.dtype),
     )(in_vmem(qkv))
+
+
+def last_rows(x):
+    streams, rows, width = x.shape
+    tall = REACH + EDGE
+    pieces = ((0, tall), (2, tall), (1, EDGE))
+
+    def body(x_ref, out_ref, sems):
+        copies = []
+        low = 0
+        for k, (s, count) in enumerate(pieces):
+            copies.append(
+                pltpu.make_async_copy(
+                    x_ref.at[s, pl.ds(rows - count, count)],
+                    out_ref.at[pl.ds(low, count)],
+                    sems.at[k],
+                )
+            )
+            low += count
+        moved(copies)
+
+    return pl.pallas_call(
+        body,
+        name="last_rows",
+        in_specs=[ANYWHERE],
+        out_specs=pl.BlockSpec(memory_space=pltpu.VMEM),
+        out_shape=pltpu.VMEM((2 * tall + EDGE, width), x.dtype),
+        scratch_shapes=[pltpu.SemaphoreType.DMA((len(pieces),))],
+    )(x)
 
 
 def by_token(blocks):
@@ -73,48 +103,66 @@
     )(in_vmem(blocks))
 
 
-def hyena_local(x, edge, short_filter, filters_back, skip):
+def hyena_local(x, tail, short_filter, filters_back, skip):
     streams, rows, width = x.shape
     short_taps = short_filter.shape[1]
     taps = filters_back.shape[1]
     cols = min(512, width)
     per_block = LANES // GW
-
-    def body(x_ref, edge_ref, short_ref, filt_ref, skip_ref, onward_ref, part_ref, gate_ref, *held):
-        ext_ref, band_ref, twice_ref = held
+    tall = REACH + EDGE
+    kept = rows - REACH
+
+    def body(x_ref, tail_ref, short_ref, filt_ref, skip_ref, onward_ref, part_ref, gate_ref, *held):
+        ext_ref, twice_ref, spread_ref = held
         row = lax.broadcasted_iota(jnp.int32, (rows, taps), 0)
         col = lax.broadcasted_iota(jnp.int32, (rows, taps), 1)
         lane_group = (lax.broadcasted_iota(jnp.int32, (rows, 2 * LANES), 1) % LANES) // GW
-        twice_ref[:rows, LANES:] = jnp.zeros((rows, LANES), jnp.bfloat16)
-        twice_ref[rows:, :LANES] = jnp.zeros((rows, LANES), jnp.bfloat16)
-        for s in range(streams):
-            ext_ref[s, :EDGE, :] = edge_ref[s].astype(jnp.float32)
-            ext_ref[s, EDGE:, :] = x_ref[s].astype(jnp.float32)
+        twice_ref[:kept, LANES:] = jnp.zeros((kept, LANES), jnp.bfloat16)
+        twice_ref[kept:, :LANES] = jnp.zeros((2 * rows - kept, LANES), jnp.bfloat16)
         for c in range(cols // LANES):
             at = pl.ds(c * LANES, LANES)
+            ext_ref[0, c, :tall, :] = tail_ref[:tall, at].astype(jnp.float32)
+            ext_ref[2, c, :tall, :] = tail_ref[tall : 2 * tall, at].astype(jnp.float32)
+            ext_ref[1, c, REACH:tall, :] = tail_ref[2 * tall :, at].astype(jnp.float32)
+            for s in range(streams):
+                ext_ref[s, c, tall:, :] = x_ref[s, :, at].astype(jnp.float32)
             out = []
-            for s in range(streams):
-                accum = None
-                for j in reversed(range(short_taps)):
-                    piece = short_ref[s, j : j + 1, at] * ext_ref[s, pl.ds(EDGE - j, rows), at]
-                    accum = piece if accum is None else accum + piece
-                out.append(accum.astype(jnp.bfloat16))
-            mixed = (out[0].astype(jnp.float32) * out[2].astype(jnp.float32)).astype(jnp.bfloat16)
-            gate_ref[:, at] = out[1]
-            twice_ref[:rows, :LANES] = mixed
-            twice_ref[rows:, LANES:] = mixed
+            for s, count in enumerate((REACH + rows, rows, REACH + rows)):
+                low = tall + rows - count
+                every = count // EDGE
+                slabs = [
+                    ext_ref[s, c, pl.ds(low + k, EDGE, stride=every), :]
+                    for k in range(1 - short_taps, every)
+                ]
+                heights = [
+                    jnp.broadcast_to(short_ref[s, j : j + 1, at], (EDGE, LANES))
+                    for j in range(short_taps)
+                ]
+                sums = []
+                for k in range(every):
+                    accum = None
+                    for j in range(short_taps):
+                        piece = heights[j] * slabs[k + short_taps - 1 - j]
+                        accum = piece if accum is None else accum + piece
+                    sums.append(accum.astype(jnp.bfloat16).astype(jnp.float32))
+                out.append(sums)
+            for k, (first, last) in enumerate(zip(out[0], out[2])):
+                spread_ref[0, c, pl.ds(k, EDGE, stride=len(out[0])), :] = first * last
+            for k, middle in enumerate(out[1]):
+                spread_ref[1, c, pl.ds(k, EDGE, stride=len(out[1])), :] = middle
+            mixed = spread_ref[0, c].astype(jnp.bfloat16)
+            gate_ref[:, at] = spread_ref[1, c, :rows].astype(jnp.bfloat16)
+            twice_ref[:kept, :LANES] = mixed[REACH : REACH + kept]
+            twice_ref[kept:, LANES:] = mixed
+            conv = None
             for g in range(per_block):
                 base = jnp.broadcast_to(filt_ref[pl.ds(c * per_block + g, 1), :], (rows, taps))
                 ring = pltpu.roll(base, 0, 1, stride=1, stride_axis=0)
-                at_g = pl.ds(g * rows, rows)
-                band_ref[at_g, :taps] = jnp.where(col > row, ring, 0.0).astype(jnp.bfloat16)
-                band_ref[at_g, taps:] = jnp.where(col <= row, ring, 0.0).astype(jnp.bfloat16)
-            every = jnp.dot(band_ref[...], twice_ref[...], preferred_element_type=jnp.float32)
-            conv = every[:rows]
-            for g in range(1, per_block):
-                conv = jnp.where(lane_group == g, every[g * rows : (g + 1) * rows], conv)
-            onward_ref[:, at] = conv[:, :LANES].astype(jnp.bfloat16)
-            part_ref[:, at] = conv[:, LANES:] + skip_ref[:, at] * mixed.astype(jnp.float32)
+                band = jnp.concatenate([jnp.where(col > row, ring, 0.0), jnp.where(col <= row, ring, 0.0)], 1).astype(jnp.bfloat16)
+                one = jnp.dot(band, twice_ref[...], preferred_element_type=jnp.float32)
+                conv = one if g == 0 else jnp.where(lane_group == g, one, conv)
+            onward_ref[:, at] = conv[:kept, :LANES].astype(jnp.bfloat16)
+            part_ref[:, at] = conv[:, LANES:] + skip_ref[:, at] * mixed[REACH:].astype(jnp.float32)
 
     wide = pl.BlockSpec((rows, cols), lambda c: (0, c))
     return pl.pallas_call(
@@ -123,28 +171,28 @@
         grid=(width // cols,),
         in_specs=[
             pl.BlockSpec((streams, rows, cols), lambda c: (0, 0, c)),
-            pl.BlockSpec((streams, EDGE, cols), lambda c: (0, 0, c)),
+            pl.BlockSpec((2 * tall + EDGE, cols), lambda c: (0, c)),
             pl.BlockSpec((streams, short_taps, cols), lambda c: (0, 0, c)),
             pl.BlockSpec((cols // GW, taps), lambda c: (c, 0)),
             pl.BlockSpec((1, cols), lambda c: (0, c)),
         ],
-        out_specs=[wide, wide, wide],
+        out_specs=[pl.BlockSpec((kept, cols), lambda c: (0, c)), wide, wide],
         out_shape=[
-            jax.ShapeDtypeStruct((rows, width), jnp.bfloat16),
+            jax.ShapeDtypeStruct((kept, width), jnp.bfloat16),
             jax.ShapeDtypeStruct((rows, width), jnp.float32),
             jax.ShapeDtypeStruct((rows, width), jnp.bfloat16),
         ],
         scratch_shapes=[
-            pltpu.VMEM((streams, rows + EDGE, cols), jnp.float32),
-            pltpu.VMEM((per_block * rows, 2 * taps), jnp.bfloat16),
+            pltpu.VMEM((streams, cols // LANES, rows + tall, LANES), jnp.float32),
             pltpu.VMEM((2 * rows, 2 * LANES), jnp.bfloat16),
+            pltpu.VMEM((2, cols // LANES, rows + REACH, LANES), jnp.float32),
         ],
         cost_estimate=pl.CostEstimate(
-            flops=4 * (width // GW) * LANES * rows * 2 * taps,
+            flops=20 * (width // GW) * LANES * rows * 2 * taps,
             transcendentals=0,
             bytes_accessed=14 * rows * width,
         ),
-    )(x, edge, short_filter, filters_back, skip)
+    )(x, tail, short_filter, filters_back, skip)
 
 
 def head_attention(blocks, scale):
@@ -230,28 +278,25 @@
 
 
 def shards(hyena_in, short_filter, mr_taps, mr_decay, skip, qkv):
-    tok_rows = hyena_in.shape[1]
     tap_count = mr_taps.shape[1]
     parts = lax.axis_size("ctx")
     scale = 1.0 / math.sqrt(HEAD)
     traded = (qkv.shape[2] // HEAD) % parts == 0
-    edge = passed_along(hyena_in[:, tok_rows - EDGE :, :], "ctx", 1)
+    tail = passed_along(last_rows(hyena_in), "ctx", 1)
     if traded:
-        outgoing, edge = lax.optimization_barrier((by_head(qkv, parts), edge))
-        blocks = lax.all_to_all(outgoing, "ctx", 0, 0, tiled=True)
+        blocks = lax.all_to_all(by_head(qkv, parts), "ctx", 0, 0, tiled=True)
     tap_pos = jnp.arange(tap_count, dtype=jnp.float32)
     filters = mr_taps * jnp.exp(-mr_decay[:, None] * tap_pos[None, :])
     filters_back = jnp.concatenate([filters[:, :1], filters[:, :0:-1]], 1)
-    onward, part, gate = hyena_local(hyena_in, edge, short_filter, filters_back, skip[None, :])
+    onward, part, gate = hyena_local(hyena_in, tail, short_filter, filters_back, skip[None, :])
     carried = passed_along(onward, "ctx", 1)
     if traded:
         done = head_attention(blocks, scale)
         attn_out = by_token(lax.all_to_all(done, "ctx", 0, 0, tiled=True))
     else:
         attn_out = gathered_attention(qkv, scale)
-    hyena_out = (gate.astype(jnp.float32) * (part + carried.astype(jnp.float32))).astype(
-        jnp.bfloat16
-    )
+    carried = jnp.pad(carried.astype(jnp.float32), ((0, REACH), (0, 0)))
+    hyena_out = (gate.astype(jnp.float32) * (part + carried)).astype(jnp.bfloat16)
     return (hyena_out, attn_out)
 
 

time: 50.5 us -> 48.9 us (0.968)
  waiting for transfers between devices: 12.3 us -> 15.3 us
  starting transfers between devices: 19.7 us -> 17.6 us
  local copies, waits for them, and re-layouts: 2.21 us -> 0.87 us
  Pallas kernels: 13.4 us -> 12.2 us
    all_to_all x1, waiting for transfers between devices: 4.89 us -> 7.28 us  [shards(): blocks = lax.all_to_all(by_head(qkv, parts), 'ctx', 0, 0, tiled=True)]
    pallas_call x1, Pallas kernels: 9.14 us -> 6.88 us  [hyena_local(): pl.pallas_call(body, name='hyena_local', grid=(width // cols,), in_specs=...]
    all_to_all x1, starting transfers between devices: 6.7 us -> 4.87 us  [shards(): blocks = lax.all_to_all(by_head(qkv, parts), 'ctx', 0, 0, tiled=True)]
    pallas_call x0 -> x1, Pallas kernels: none -> 1.04 us  [last_rows(): pl.pallas_call(body, name='last_rows', in_specs=[ANYWHERE], out_specs=pl....]
    slice x1 -> x0, local copies, waits for them, and re-layouts: 0.9 us -> none  [shards(): edge = passed_along(hyena_in[:, tok_rows - EDGE:, :], 'ctx', 1)]
    all_to_all x1, waiting for transfers between devices: 7.37 us -> 8 us  [shards(): attn_out = by_token(lax.all_to_all(done, 'ctx', 0, 0, tiled=True))]
  transfers between devices with their start and end apart: 4 -> 4, of which waited for: 2 -> 2; matrix products, arithmetic and copies ran while one was open for 4% -> 4% of each run, Pallas kernels for 25% -> 21%
where the time goes in v4:
time: 48.9 us; the launch traced here: 48.5 us
  starting transfers between devices  17.6 us (36%)
  waiting for transfers between devices  15.3 us (31%)
  Pallas kernels  12.2 us (25%)
  other arithmetic  1.8 us (4%)
  local copies, waits for them, and re-layouts  0.87 us (2%)
  between operations  0.74 us (2%)
    ppermute x2, starting transfers between devices, passed_along(): return lax.ppermute(block, axis, route)  9.09 us
    all_to_all x1, waiting for transfers between devices, shards(): attn_out = by_token(lax.all_to_all(done, 'ctx', 0, 0, tiled=True))  8 us
    all_to_all x1, waiting for transfers between devices, shards(): blocks = lax.all_to_all(by_head(qkv, parts), 'ctx', 0, 0, tiled=True)  7.28 us
    pallas_call x1, Pallas kernels, hyena_local(): pl.pallas_call(body, name='hyena_local', grid=(width // cols,), in_specs=...  6.88 us
    all_to_all x1, starting transfers between devices, shards(): blocks = lax.all_to_all(by_head(qkv, parts), 'ctx', 0, 0, tiled=True)  4.87 us
    all_to_all x1, starting transfers between devices, shards(): attn_out = by_token(lax.all_to_all(done, 'ctx', 0, 0, tiled=True))  3.64 us
    pallas_call x1, Pallas kernels, head_attention(): pl.pallas_call(body, name='head_attention', in_specs=[pl.BlockSpec(memory...  2.44 us
    pallas_call x1, Pallas kernels, by_head(): pl.pallas_call(body, name='by_head', in_specs=[pl.BlockSpec(memory_space=...  1.06 us
  transfers between devices with their start and end apart: 4, of which 2 were waited for; matrix products, arithmetic and copies ran while one was open for 4% of the time, Pallas kernels for 21%

profile of v4, /device:TPU:0, one launch (start us, length us, event | category | flops | bytes accessed | tf_op | source)
XLA Modules:
  0.0 48.5 jit_solution(5559996575156354558)
XLA Ops:
  0.6 0.0 copy-start
  0.6 1.0 %last_rows.1 = bf16[56,2048]{1,0:T(8,128)(2,1)S(1)} custom-call(bf16[3,128,2048]{2,1,0:T(8,128)(2,1)} %x_ref.3), custom_call_target="tpu_custom_call" | custom-call | tf_op jit(solution)/shard_map/last_rows/pallas_call | solution.py:73
  1.7 0.0 copy-start.5
  1.7 0.0 copy-start.3
  1.7 5.0 %collective-permute-start = (bf16[56,2048]{1,0:T(8,128)(2,1)S(1)}, bf16[56,2048]{1,0:T(8,128)(2,1)S(1)}, u32[]{:S(2)}, u32[]{:S(2)}) collective-permute-start(bf16[56,2048]{1,0:T(8,128)(2,1)S(1)} %last_rows.1), channel_id=1, source_target_pairs={{0,2},{2,4},{4,6},{6,8},{8,10},{10,12},{12,14},{1,3},{3,5},{5,7},{... | collective-permute-start | bytes 688136 | tf_op jit(solution)/shard_map/ppermute | solution.py:20
  6.7 0.0 copy-done
  6.7 1.1 %by_head.1 = bf16[8,3,128,128]{3,2,1,0:T(8,128)(2,1)} custom-call(bf16[3,128,1024]{2,1,0:T(8,128)(2,1)S(1)} %copy-done), custom_call_target="tpu_custom_call" | custom-call | tf_op jit(solution)/shard_map/by_head/pallas_call | solution.py:45
  7.8 4.9 %all-to-all-start = ((bf16[8,3,128,128]{3,2,1,0:T(8,128)(2,1)}), bf16[8,3,128,128]{3,2,1,0:T(8,128)(2,1)S(1)}, u32[]{:S(2)}, u32[]{:S(2)}) async-start(bf16[8,3,128,128]{3,2,1,0:T(8,128)(2,1)} %by_head.1), calls=%async_computation | async-start | bytes 1572864 | tf_op jit(solution)/shard_map/all_to_all | solution.py:287
  12.7 0.0 copy-done.5
  12.7 0.0 copy-done.3
  12.7 0.1 exponential_multiply_fusion
  12.8 0.1 slice.9
  12.9 0.1 rev.3
  13.0 0.7 %pad_maximum_fusion.filt_ref = f32[128,128]{1,0:T(8,128)} fusion(f32[128,127]{1,0:T(8,128)S(1)} %rev.3, f32[128,1]{1,0:T(8,128)S(1)} %bitcast.2), kind=kLoop, calls=%fused_computation.1 | loop fusion | flops 16384 | bytes 131072 | tf_op jit(solution)/shard_map/concatenate | solution.py:290
  13.7 0.0 collective-permute-done.tail_ref
  13.7 0.0 copy-start.4
  13.7 0.7 %copy-done.4 = bf16[56,2048]{1,0:T(8,128)(2,1)} copy-done((bf16[56,2048]{1,0:T(8,128)(2,1)}, bf16[56,2048]{1,0:T(8,128)(2,1)S(1)}, u32[]{:S(2)}) %copy-start.4) | copy-done | bytes 229400
  14.4 6.9 %hyena_local.1 = (bf16[112,2048]{1,0:T(8,128)(2,1)}, f32[128,2048]{1,0:T(8,128)}, bf16[128,2048]{1,0:T(8,128)(2,1)}) custom-call(bf16[3,128,2048]{2,1,0:T(8,128)(2,1)} %x_ref.3, bf16[56,2048]{1,0:T(8,128)(2,1)} %copy-done.4, f32[3,7,2048]{2,1,0:T(8,128)} %short_ref.1, f32[128,128]{1,0:T(8,128)} %pad_maximum_fusion.filt_ref, f32[1,2048]{1,0:T(1,128)} %bitcast.3), custom_call_target="tpu_custom_call" | custom-call | flops 10737418240 | bytes 3670016 | tf_op jit(solution)/shard_map/hyena_local/pallas_call | solution.py:168
  21.3 0.0 copy-start.1
  21.3 0.0 copy-start.2
  21.3 4.1 %collective-permute-start.1 = (bf16[112,2048]{1,0:T(8,128)(2,1)}, bf16[112,2048]{1,0:T(8,128)(2,1)S(1)}, u32[]{:S(2)}, u32[]{:S(2)}) collective-permute-start(bf16[112,2048]{1,0:T(8,128)(2,1)} %get-tuple-element.7), channel_id=1, source_target_pairs={{0,2},{2,4},{4,6},{6,8},{8,10},{10,12},{12,14},{1,3},{3,5},{5,7},{... | collective-permute-start | bytes 1376264 | tf_op jit(solution)/shard_map/ppermute | solution.py:20
  25.4 7.3 %all-to-all-done.in_ref = bf16[8,3,128,128]{3,2,1,0:T(8,128)(2,1)S(1)} async-done(((bf16[8,3,128,128]{3,2,1,0:T(8,128)(2,1)}), bf16[8,3,128,128]{3,2,1,0:T(8,128)(2,1)S(1)}, u32[]{:S(2)}, u32[]{:S(2)}) %all-to-all-start) | async-done | bytes 786464 | tf_op jit(solution)/shard_map/all_to_all | solution.py:287
  32.6 2.4 %head_attention.1 = bf16[8,128,128]{2,1,0:T(8,128)(2,1)} custom-call(bf16[8,3,128,128]{3,2,1,0:T(8,128)(2,1)S(1)} %all-to-all-done.in_ref), custom_call_target="tpu_custom_call" | custom-call | flops 268435456 | bytes 1048576 | tf_op jit(solution)/shard_map/head_attention/pallas_call | solution.py:234
  35.1 3.6 %all-to-all-start.1 = ((bf16[8,128,128]{2,1,0:T(8,128)(2,1)}), bf16[8,128,128]{2,1,0:T(8,128)(2,1)S(1)}, u32[]{:S(2)}, u32[]{:S(2)}) async-start(bf16[8,128,128]{2,1,0:T(8,128)(2,1)} %head_attention.1), calls=%async_computation.1 | async-start | bytes 524288 | tf_op jit(solution)/shard_map/all_to_all | solution.py:295
  38.7 0.0 collective-permute-done.1
  38.7 0.0 copy-done.1
  38.7 0.0 copy-done.2
  38.8 1.0 %multiply_convert_fusion = bf16[128,2048]{1,0:T(8,128)(2,1)} fusion(f32[128,2048]{1,0:T(8,128)S(1)} %copy-done.1, bf16[128,2048]{1,0:T(8,128)(2,1)S(1)} %copy-done.2, bf16[112,2048]{1,0:T(8,128)(2,1)S(1)} %collective-permute-done.1), kind=kLoop, calls=%fused_computation | loop fusion | flops 1310720 | bytes 2555904 | tf_op jit(solution)/shard_map/convert_element_type | solution.py:299
  39.7 8.0 %all-to-all-done.1.in_ref = bf16[8,128,128]{2,1,0:T(8,128)(2,1)S(1)} async-done(((bf16[8,128,128]{2,1,0:T(8,128)(2,1)}), bf16[8,128,128]{2,1,0:T(8,128)(2,1)S(1)}, u32[]{:S(2)}, u32[]{:S(2)}) %all-to-all-start.1) | async-done | bytes 262176 | tf_op jit(solution)/shard_map/all_to_all | solution.py:295
  47.7 0.8 %by_token.1 = bf16[128,1024]{1,0:T(8,128)(2,1)} custom-call(bf16[8,128,128]{2,1,0:T(8,128)(2,1)S(1)} %all-to-all-done.1.in_ref), custom_call_target="tpu_custom_call" | custom-call | tf_op jit(solution)/shard_map/by_token/pallas_call | solution.py:96
  (1 shorter events, 0.0 us)
Async XLA Ops:
  0.6 6.1 %copy-start = (bf16[3,128,1024]{2,1,0:T(8,128)(2,1)S(1)}, bf16[3,128,1024]{2,1,0:T(8,128)(2,1)}, u32[]{:S(2)}) copy-start(bf16[3,128,1024]{2,1,0:T(8,128)(2,1)} %qkv_ref.1) | copy-start | bytes 2359300
  1.7 11.0 %copy-start.5 = (f32[128]{0:T(128)S(1)}, f32[128]{0:T(128)}, u32[]{:S(2)}) copy-start(f32[128]{0:T(128)} %param.9) | copy-start | bytes 1540
  1.7 11.0 %copy-start.3 = (f32[128,128]{1,0:T(8,128)S(1)}, f32[128,128]{1,0:T(8,128)}, u32[]{:S(2)}) copy-start(f32[128,128]{1,0:T(8,128)} %param.8) | copy-start | bytes 196612
  1.7 12.0 %collective-permute-start = (bf16[56,2048]{1,0:T(8,128)(2,1)S(1)}, bf16[56,2048]{1,0:T(8,128)(2,1)S(1)}, u32[]{:S(2)}, u32[]{:S(2)}) collective-permute-start(bf16[56,2048]{1,0:T(8,128)(2,1)S(1)} %last_rows.1), channel_id=1, source_target_pairs={{0,2},{2,4},{4,6},{6,8},{8,10},{10,12},{12,14},{1,3},{3,5},{5,7},{... | collective-permute-start | bytes 688136 | tf_op jit(solution)/shard_map/ppermute | solution.py:20
  7.8 24.8 %all-to-all-start = ((bf16[8,3,128,128]{3,2,1,0:T(8,128)(2,1)}), bf16[8,3,128,128]{3,2,1,0:T(8,128)(2,1)S(1)}, u32[]{:S(2)}, u32[]{:S(2)}) async-start(bf16[8,3,128,128]{3,2,1,0:T(8,128)(2,1)} %by_head.1), calls=%async_computation | async-start | bytes 1572864 | tf_op jit(solution)/shard_map/all_to_all | solution.py:287
  13.7 0.7 %copy-start.4 = (bf16[56,2048]{1,0:T(8,128)(2,1)}, bf16[56,2048]{1,0:T(8,128)(2,1)S(1)}, u32[]{:S(2)}) copy-start(bf16[56,2048]{1,0:T(8,128)(2,1)S(1)} %collective-permute-done.tail_ref) | copy-start | bytes 688132
  21.3 17.5 %copy-start.1 = (f32[128,2048]{1,0:T(8,128)S(1)}, f32[128,2048]{1,0:T(8,128)}, u32[]{:S(2)}) copy-start(f32[128,2048]{1,0:T(8,128)} %get-tuple-element.6) | copy-start | bytes 3145732
  21.3 17.5 %copy-start.2 = (bf16[128,2048]{1,0:T(8,128)(2,1)S(1)}, bf16[128,2048]{1,0:T(8,128)(2,1)}, u32[]{:S(2)}) copy-start(bf16[128,2048]{1,0:T(8,128)(2,1)} %get-tuple-element.5) | copy-start | bytes 1572868
  21.3 17.5 %collective-permute-start.1 = (bf16[112,2048]{1,0:T(8,128)(2,1)}, bf16[112,2048]{1,0:T(8,128)(2,1)S(1)}, u32[]{:S(2)}, u32[]{:S(2)}) collective-permute-start(bf16[112,2048]{1,0:T(8,128)(2,1)} %get-tuple-element.7), channel_id=1, source_target_pairs={{0,2},{2,4},{4,6},{6,8},{8,10},{10,12},{12,14},{1,3},{3,5},{5,7},{... | collective-permute-start | bytes 1376264 | tf_op jit(solution)/shard_map/ppermute | solution.py:20
  35.1 12.6 %all-to-all-start.1 = ((bf16[8,128,128]{2,1,0:T(8,128)(2,1)}), bf16[8,128,128]{2,1,0:T(8,128)(2,1)S(1)}, u32[]{:S(2)}, u32[]{:S(2)}) async-start(bf16[8,128,128]{2,1,0:T(8,128)(2,1)} %head_attention.1), calls=%async_computation.1 | async-start | bytes 524288 | tf_op jit(solution)/shard_map/all_to_all | solution.py:295

commit v5 on v4

--- a/solution.py
+++ b/solution.py
@@ -12,6 +12,8 @@
 LANES = 128
 EDGE = 8
 REACH = 16
+ORDER_IN = (0, 3, 2, 6, 7, 5, 4, 1)
+ORDER_OUT = (0, 6, 3, 4, 1, 7, 5, 2)
 
 
 def passed_along(block, axis, distance):
@@ -34,20 +36,34 @@
         copy.wait()
 
 
-def by_head(qkv, parts):
+def visiting(parts, order):
+    return order if len(order) == parts else tuple(range(parts))
+
+
+def by_head(qkv, order):
+    parts = len(order)
     streams, rows, full = qkv.shape
     width = full // parts
 
-    def body(qkv_ref, out_ref):
+    def body(qkv_ref, out_ref, held_ref, sems):
+        copies = []
         for p in range(parts):
-            out_ref[p] = qkv_ref[:, :, pl.ds(p * width, width)]
+            held_ref[p] = qkv_ref[:, :, pl.ds(order[p] * width, width)]
+            copies.append(pltpu.make_async_copy(held_ref.at[p], out_ref.at[p], sems.at[p]))
+            copies[-1].start()
+        for copy in copies:
+            copy.wait()
 
     return pl.pallas_call(
         body,
         name="by_head",
         in_specs=[pl.BlockSpec(memory_space=pltpu.VMEM)],
-        out_specs=pl.BlockSpec(memory_space=pltpu.VMEM),
-        out_shape=pltpu.VMEM((parts, streams, rows, width), qkv.dtype),
+        out_specs=ANYWHERE,
+        out_shape=jax.ShapeDtypeStruct((parts, streams, rows, width), qkv.dtype),
+        scratch_shapes=[
+            pltpu.VMEM((parts, streams, rows, width), qkv.dtype),
+            pltpu.SemaphoreType.DMA((parts,)),
+        ],
     )(in_vmem(qkv))
 
 
@@ -80,14 +96,14 @@
     )(x)
 
 
-def by_token(blocks):
+def by_token(blocks, order):
     parts, rows, width = blocks.shape
 
     def body(in_ref, out_ref, sems):
         moved(
             [
                 pltpu.make_async_copy(
-                    in_ref.at[p], out_ref.at[:, pl.ds(p * width, width)], sems.at[p]
+                    in_ref.at[p], out_ref.at[:, pl.ds(order[p] * width, width)], sems.at[p]
                 )
                 for p in range(parts)
             ]
@@ -195,22 +211,29 @@
     )(x, tail, short_filter, filters_back, skip)
 
 
-def head_attention(blocks, scale):
+def head_attention(blocks, order, order_out, scale):
     parts, _, rows, width = blocks.shape
     step = 2 if parts % 2 == 0 else 1
     q_rows = step * rows
-
-    def body(in_ref, out_ref):
+    place = [order.index(token) for token in range(parts)]
+    place_out = [order_out.index(token) for token in range(parts)]
+
+    def body(in_ref, out_ref, held_ref, sems):
+        copies = []
         row = lax.broadcasted_iota(jnp.int32, (q_rows, q_rows), 0)
         col = lax.broadcasted_iota(jnp.int32, (q_rows, q_rows), 1)
         keep = col <= row
+
+        def stacked(s, at, tokens):
+            return jnp.concatenate([in_ref[place[token], s, :, at] for token in tokens], 0)
+
         for h in range(width // HEAD):
             at = pl.ds(h * HEAD, HEAD)
-            for b in range(parts // step):
+            for b in reversed(range(parts // step)):
                 upto = (b + 1) * step
-                query = in_ref[b * step : upto, 0, :, at].reshape(q_rows, HEAD)
-                keys = in_ref[:upto, 1, :, at].reshape(upto * rows, HEAD)
-                values = in_ref[:upto, 2, :, at].reshape(upto * rows, HEAD)
+                query = stacked(0, at, range(b * step, upto))
+                keys = stacked(1, at, range(upto))
+                values = stacked(2, at, range(upto))
                 scores = lax.dot_general(
                     query, keys, (((1,), (1,)), ((), ())), preferred_element_type=jnp.float32
                 )
@@ -226,16 +249,30 @@
                 summed = jnp.dot(
                     weights.astype(jnp.bfloat16), values, preferred_element_type=jnp.float32
                 )
-                out_ref[b * step : upto, :, at] = (
-                    (summed / total).astype(jnp.bfloat16).reshape(step, rows, HEAD)
-                )
+                done = (summed / total).astype(jnp.bfloat16)
+                for k in range(step):
+                    token = b * step + k
+                    held_ref[place_out[token], :, at] = done[k * rows : (k + 1) * rows]
+                    if h == width // HEAD - 1:
+                        copies.append(
+                            pltpu.make_async_copy(
+                                held_ref.at[place_out[token]], out_ref.at[place_out[token]], sems.at[token]
+                            )
+                        )
+                        copies[-1].start()
+        for copy in copies:
+            copy.wait()
 
     tokens = parts * rows
     return pl.pallas_call(
         body,
         name="head_attention",
         in_specs=[pl.BlockSpec(memory_space=pltpu.VMEM)],
-        out_specs=pl.BlockSpec(memory_space=pltpu.VMEM),
+        out_specs=ANYWHERE,
+        scratch_shapes=[
+            pltpu.VMEM((parts, rows, width), jnp.bfloat16),
+            pltpu.SemaphoreType.DMA((parts,)),
+        ],
         out_shape=jax.ShapeDtypeStruct((parts, rows, width), jnp.bfloat16),
         cost_estimate=pl.CostEstimate(
             flops=2 * tokens * tokens * width,
@@ -277,22 +314,27 @@
     return jnp.concatenate(out_list, 1)
 
 
+def traded(blocks, order):
+    return lax.all_to_all(blocks, "ctx", 0, 0, tiled=True, axis_index_groups=[list(order)])
+
+
 def shards(hyena_in, short_filter, mr_taps, mr_decay, skip, qkv):
     tap_count = mr_taps.shape[1]
     parts = lax.axis_size("ctx")
     scale = 1.0 / math.sqrt(HEAD)
-    traded = (qkv.shape[2] // HEAD) % parts == 0
+    whole_heads = (qkv.shape[2] // HEAD) % parts == 0
     tail = passed_along(last_rows(hyena_in), "ctx", 1)
-    if traded:
-        blocks = lax.all_to_all(by_head(qkv, parts), "ctx", 0, 0, tiled=True)
+    if whole_heads:
+        order, order_out = visiting(parts, ORDER_IN), visiting(parts, ORDER_OUT)
+        blocks = traded(by_head(qkv, order), order)
     tap_pos = jnp.arange(tap_count, dtype=jnp.float32)
     filters = mr_taps * jnp.exp(-mr_decay[:, None] * tap_pos[None, :])
     filters_back = jnp.concatenate([filters[:, :1], filters[:, :0:-1]], 1)
     onward, part, gate = hyena_local(hyena_in, tail, short_filter, filters_back, skip[None, :])
     carried = passed_along(onward, "ctx", 1)
-    if traded:
-        done = head_attention(blocks, scale)
-        attn_out = by_token(lax.all_to_all(done, "ctx", 0, 0, tiled=True))
+    if whole_heads:
+        done = head_attention(blocks, order, order_out, scale)
+        attn_out = by_token(traded(done, order_out), order_out)
     else:
         attn_out = gathered_attention(qkv, scale)
     carried = jnp.pad(carried.astype(jnp.float32), ((0, REACH), (0, 0)))

time: 48.9 us -> 46.8 us (0.957)
  waiting for transfers between devices: 15.3 us -> 11.3 us
  starting transfers between devices: 17.6 us -> 19.6 us
    all_to_all x2, waiting for transfers between devices: 15.3 us -> 11.3 us  [traded(): lax.all_to_all(blocks, 'ctx', 0, 0, tiled=True, axis_index_groups=[list(o...]
    all_to_all x2, starting transfers between devices: 8.51 us -> 10.5 us  [traded(): lax.all_to_all(blocks, 'ctx', 0, 0, tiled=True, axis_index_groups=[list(o...]
  transfers between devices with their start and end apart: 4 -> 4, of which waited for: 2 -> 2; matrix products, arithmetic and copies ran while one was open for 4% -> 4% of each run, Pallas kernels for 21% -> 22%
where the time goes in v5:
time: 46.8 us; the launch traced here: 46.4 us
  starting transfers between devices  19.6 us (42%)
  Pallas kernels  12 us (26%)
  waiting for transfers between devices  11.3 us (24%)
  other arithmetic  1.8 us (4%)
  local copies, waits for them, and re-layouts  0.87 us (2%)
  between operations  0.76 us (2%)
    all_to_all x2, waiting for transfers between devices, traded(): lax.all_to_all(blocks, 'ctx', 0, 0, tiled=True, axis_index_groups=[list(o...  11.3 us
    all_to_all x2, starting transfers between devices, traded(): lax.all_to_all(blocks, 'ctx', 0, 0, tiled=True, axis_index_groups=[list(o...  10.5 us
    ppermute x2, starting transfers between devices, passed_along(): return lax.ppermute(block, axis, route)  9.1 us
    pallas_call x1, Pallas kernels, hyena_local(): pl.pallas_call(body, name='hyena_local', grid=(width // cols,), in_specs=...  6.88 us
    pallas_call x1, Pallas kernels, head_attention(): pl.pallas_call(body, name='head_attention', in_specs=[pl.BlockSpec(memory...  2.35 us
    pallas_call x1, Pallas kernels, last_rows(): pl.pallas_call(body, name='last_rows', in_specs=[ANYWHERE], out_specs=pl....  1.04 us
    pallas_call x1, Pallas kernels, by_head(): pl.pallas_call(body, name='by_head', in_specs=[pl.BlockSpec(memory_space=...  1.02 us
    convert_element_type x1, other arithmetic, shards(): (gate.astype(jnp.float32) * (part + carried)).astype(jnp.bfloat16)  0.98 us
  transfers between devices with their start and end apart: 4, of which 2 were waited for; matrix products, arithmetic and copies ran while one was open for 4% of the time, Pallas kernels for 22%

profile of v5, /device:TPU:0, one launch (start us, length us, event | category | flops | bytes accessed | tf_op | source)
XLA Modules:
  0.0 46.4 jit_solution(11719442902081011298)
XLA Ops:
  0.6 0.0 copy-start
  0.6 1.0 %last_rows.1 = bf16[56,2048]{1,0:T(8,128)(2,1)S(1)} custom-call(bf16[3,128,2048]{2,1,0:T(8,128)(2,1)} %x_ref.3), custom_call_target="tpu_custom_call" | custom-call | tf_op jit(solution)/shard_map/last_rows/pallas_call | solution.py:89
  1.7 0.0 copy-start.5
  1.7 0.0 copy-start.3
  1.7 5.0 %collective-permute-start = (bf16[56,2048]{1,0:T(8,128)(2,1)S(1)}, bf16[56,2048]{1,0:T(8,128)(2,1)S(1)}, u32[]{:S(2)}, u32[]{:S(2)}) collective-permute-start(bf16[56,2048]{1,0:T(8,128)(2,1)S(1)} %last_rows.1), channel_id=1, source_target_pairs={{0,2},{2,4},{4,6},{6,8},{8,10},{10,12},{12,14},{1,3},{3,5},{5,7},{... | collective-permute-start | bytes 688136 | tf_op jit(solution)/shard_map/ppermute | solution.py:22
  6.7 0.0 copy-done
  6.7 1.0 %by_head.1 = bf16[8,3,128,128]{3,2,1,0:T(8,128)(2,1)} custom-call(bf16[3,128,1024]{2,1,0:T(8,128)(2,1)S(1)} %copy-done), custom_call_target="tpu_custom_call" | custom-call | tf_op jit(solution)/shard_map/by_head/pallas_call | solution.py:57
  7.8 4.9 %all-to-all-start = ((bf16[8,3,128,128]{3,2,1,0:T(8,128)(2,1)}), bf16[8,3,128,128]{3,2,1,0:T(8,128)(2,1)S(1)}, u32[]{:S(2)}, u32[]{:S(2)}) async-start(bf16[8,3,128,128]{3,2,1,0:T(8,128)(2,1)} %by_head.1), calls=%async_computation | async-start | bytes 1572864 | tf_op jit(solution)/shard_map/all_to_all | solution.py:318
  12.7 0.0 copy-done.5
  12.7 0.0 copy-done.3
  12.7 0.1 exponential_multiply_fusion
  12.8 0.1 slice.9
  12.9 0.1 rev.3
  12.9 0.7 %pad_maximum_fusion.filt_ref = f32[128,128]{1,0:T(8,128)} fusion(f32[128,127]{1,0:T(8,128)S(1)} %rev.3, f32[128,1]{1,0:T(8,128)S(1)} %bitcast.2), kind=kLoop, calls=%fused_computation.1 | loop fusion | flops 16384 | bytes 131072 | tf_op jit(solution)/shard_map/concatenate | solution.py:332
  13.7 0.0 collective-permute-done.tail_ref
  13.7 0.0 copy-start.4
  13.7 0.7 %copy-done.4 = bf16[56,2048]{1,0:T(8,128)(2,1)} copy-done((bf16[56,2048]{1,0:T(8,128)(2,1)}, bf16[56,2048]{1,0:T(8,128)(2,1)S(1)}, u32[]{:S(2)}) %copy-start.4) | copy-done | bytes 229400
  14.4 6.9 %hyena_local.1 = (bf16[112,2048]{1,0:T(8,128)(2,1)}, f32[128,2048]{1,0:T(8,128)}, bf16[128,2048]{1,0:T(8,128)(2,1)}) custom-call(bf16[3,128,2048]{2,1,0:T(8,128)(2,1)} %x_ref.3, bf16[56,2048]{1,0:T(8,128)(2,1)} %copy-done.4, f32[3,7,2048]{2,1,0:T(8,128)} %short_ref.1, f32[128,128]{1,0:T(8,128)} %pad_maximum_fusion.filt_ref, f32[1,2048]{1,0:T(1,128)} %bitcast.3), custom_call_target="tpu_custom_call" | custom-call | flops 10737418240 | bytes 3670016 | tf_op jit(solution)/shard_map/hyena_local/pallas_call | solution.py:184
  21.2 0.0 copy-start.1
  21.2 0.0 copy-start.2
  21.3 4.1 %collective-permute-start.1 = (bf16[112,2048]{1,0:T(8,128)(2,1)}, bf16[112,2048]{1,0:T(8,128)(2,1)S(1)}, u32[]{:S(2)}, u32[]{:S(2)}) collective-permute-start(bf16[112,2048]{1,0:T(8,128)(2,1)} %get-tuple-element.7), channel_id=1, source_target_pairs={{0,2},{2,4},{4,6},{6,8},{8,10},{10,12},{12,14},{1,3},{3,5},{5,7},{... | collective-permute-start | bytes 1376264 | tf_op jit(solution)/shard_map/ppermute | solution.py:22
  25.3 5.0 %all-to-all-done.in_ref = bf16[8,3,128,128]{3,2,1,0:T(8,128)(2,1)S(1)} async-done(((bf16[8,3,128,128]{3,2,1,0:T(8,128)(2,1)}), bf16[8,3,128,128]{3,2,1,0:T(8,128)(2,1)S(1)}, u32[]{:S(2)}, u32[]{:S(2)}) %all-to-all-start) | async-done | bytes 786464 | tf_op jit(solution)/shard_map/all_to_all | solution.py:318
  30.3 2.3 %head_attention.1 = bf16[8,128,128]{2,1,0:T(8,128)(2,1)} custom-call(bf16[8,3,128,128]{3,2,1,0:T(8,128)(2,1)S(1)} %all-to-all-done.in_ref), custom_call_target="tpu_custom_call" | custom-call | flops 268435456 | bytes 1048576 | tf_op jit(solution)/shard_map/head_attention/pallas_call | solution.py:267
  32.7 5.6 %all-to-all-start.1 = ((bf16[8,128,128]{2,1,0:T(8,128)(2,1)}), bf16[8,128,128]{2,1,0:T(8,128)(2,1)S(1)}, u32[]{:S(2)}, u32[]{:S(2)}) async-start(bf16[8,128,128]{2,1,0:T(8,128)(2,1)} %head_attention.1), calls=%async_computation.1 | async-start | bytes 524288 | tf_op jit(solution)/shard_map/all_to_all | solution.py:318
  38.3 0.0 collective-permute-done.1
  38.3 0.0 copy-done.1
  38.4 0.0 copy-done.2
  38.4 1.0 %multiply_convert_fusion = bf16[128,2048]{1,0:T(8,128)(2,1)} fusion(f32[128,2048]{1,0:T(8,128)S(1)} %copy-done.1, bf16[128,2048]{1,0:T(8,128)(2,1)S(1)} %copy-done.2, bf16[112,2048]{1,0:T(8,128)(2,1)S(1)} %collective-permute-done.1), kind=kLoop, calls=%fused_computation | loop fusion | flops 1310720 | bytes 2555904 | tf_op jit(solution)/shard_map/convert_element_type | solution.py:341
  39.3 6.3 %all-to-all-done.1.in_ref = bf16[8,128,128]{2,1,0:T(8,128)(2,1)S(1)} async-done(((bf16[8,128,128]{2,1,0:T(8,128)(2,1)}), bf16[8,128,128]{2,1,0:T(8,128)(2,1)S(1)}, u32[]{:S(2)}, u32[]{:S(2)}) %all-to-all-start.1) | async-done | bytes 262176 | tf_op jit(solution)/shard_map/all_to_all | solution.py:318
  45.6 0.8 %by_token.1 = bf16[128,1024]{1,0:T(8,128)(2,1)} custom-call(bf16[8,128,128]{2,1,0:T(8,128)(2,1)S(1)} %all-to-all-done.1.in_ref), custom_call_target="tpu_custom_call" | custom-call | tf_op jit(solution)/shard_map/by_token/pallas_call | solution.py:112
  (1 shorter events, 0.0 us)
Async XLA Ops:
  0.6 6.1 %copy-start = (bf16[3,128,1024]{2,1,0:T(8,128)(2,1)S(1)}, bf16[3,128,1024]{2,1,0:T(8,128)(2,1)}, u32[]{:S(2)}) copy-start(bf16[3,128,1024]{2,1,0:T(8,128)(2,1)} %qkv_ref.1) | copy-start | bytes 2359300
  1.7 11.0 %copy-start.5 = (f32[128]{0:T(128)S(1)}, f32[128]{0:T(128)}, u32[]{:S(2)}) copy-start(f32[128]{0:T(128)} %param.9) | copy-start | bytes 1540
  1.7 11.0 %copy-start.3 = (f32[128,128]{1,0:T(8,128)S(1)}, f32[128,128]{1,0:T(8,128)}, u32[]{:S(2)}) copy-start(f32[128,128]{1,0:T(8,128)} %param.8) | copy-start | bytes 196612
  1.7 12.0 %collective-permute-start = (bf16[56,2048]{1,0:T(8,128)(2,1)S(1)}, bf16[56,2048]{1,0:T(8,128)(2,1)S(1)}, u32[]{:S(2)}, u32[]{:S(2)}) collective-permute-start(bf16[56,2048]{1,0:T(8,128)(2,1)S(1)} %last_rows.1), channel_id=1, source_target_pairs={{0,2},{2,4},{4,6},{6,8},{8,10},{10,12},{12,14},{1,3},{3,5},{5,7},{... | collective-permute-start | bytes 688136 | tf_op jit(solution)/shard_map/ppermute | solution.py:22
  7.8 22.6 %all-to-all-start = ((bf16[8,3,128,128]{3,2,1,0:T(8,128)(2,1)}), bf16[8,3,128,128]{3,2,1,0:T(8,128)(2,1)S(1)}, u32[]{:S(2)}, u32[]{:S(2)}) async-start(bf16[8,3,128,128]{3,2,1,0:T(8,128)(2,1)} %by_head.1), calls=%async_computation | async-start | bytes 1572864 | tf_op jit(solution)/shard_map/all_to_all | solution.py:318
  13.7 0.7 %copy-start.4 = (bf16[56,2048]{1,0:T(8,128)(2,1)}, bf16[56,2048]{1,0:T(8,128)(2,1)S(1)}, u32[]{:S(2)}) copy-start(bf16[56,2048]{1,0:T(8,128)(2,1)S(1)} %collective-permute-done.tail_ref) | copy-start | bytes 688132
  21.2 17.1 %copy-start.1 = (f32[128,2048]{1,0:T(8,128)S(1)}, f32[128,2048]{1,0:T(8,128)}, u32[]{:S(2)}) copy-start(f32[128,2048]{1,0:T(8,128)} %get-tuple-element.6) | copy-start | bytes 3145732
  21.2 17.1 %copy-start.2 = (bf16[128,2048]{1,0:T(8,128)(2,1)S(1)}, bf16[128,2048]{1,0:T(8,128)(2,1)}, u32[]{:S(2)}) copy-start(bf16[128,2048]{1,0:T(8,128)(2,1)} %get-tuple-element.5) | copy-start | bytes 1572868
  21.3 17.1 %collective-permute-start.1 = (bf16[112,2048]{1,0:T(8,128)(2,1)}, bf16[112,2048]{1,0:T(8,128)(2,1)S(1)}, u32[]{:S(2)}, u32[]{:S(2)}) collective-permute-start(bf16[112,2048]{1,0:T(8,128)(2,1)} %get-tuple-element.7), channel_id=1, source_target_pairs={{0,2},{2,4},{4,6},{6,8},{8,10},{10,12},{12,14},{1,3},{3,5},{5,7},{... | collective-permute-start | bytes 1376264 | tf_op jit(solution)/shard_map/ppermute | solution.py:22
  32.7 12.9 %all-to-all-start.1 = ((bf16[8,128,128]{2,1,0:T(8,128)(2,1)}), bf16[8,128,128]{2,1,0:T(8,128)(2,1)S(1)}, u32[]{:S(2)}, u32[]{:S(2)}) async-start(bf16[8,128,128]{2,1,0:T(8,128)(2,1)} %head_attention.1), calls=%async_computation.1 | async-start | bytes 524288 | tf_op jit(solution)/shard_map/all_to_all | solution.py:318

commit v6 on v5

--- a/solution.py
+++ b/solution.py
@@ -12,7 +12,7 @@
 LANES = 128
 EDGE = 8
 REACH = 16
-ORDER_IN = (0, 3, 2, 6, 7, 5, 4, 1)
+ORDER_IN = (0, 6, 3, 4, 1, 7, 5, 2)
 ORDER_OUT = (0, 6, 3, 4, 1, 7, 5, 2)
 
 
@@ -229,26 +229,30 @@
 
         for h in range(width // HEAD):
             at = pl.ds(h * HEAD, HEAD)
-            for b in reversed(range(parts // step)):
+            spans = list(reversed(range(parts // step)))
+
+            def scored(b):
                 upto = (b + 1) * step
-                query = stacked(0, at, range(b * step, upto))
-                keys = stacked(1, at, range(upto))
-                values = stacked(2, at, range(upto))
                 scores = lax.dot_general(
-                    query, keys, (((1,), (1,)), ((), ())), preferred_element_type=jnp.float32
+                    stacked(0, at, range(b * step, upto)),
+                    stacked(1, at, range(upto)),
+                    (((1,), (1,)), ((), ())),
+                    preferred_element_type=jnp.float32,
                 )
                 low = b * q_rows
                 edge_scores = jnp.where(keep, scores[:, low:], -1e30)
                 if b:
-                    scores = jnp.concatenate([scores[:, :low], edge_scores], 1)
-                else:
-                    scores = edge_scores
+                    return jnp.concatenate([scores[:, :low], edge_scores], 1)
+                return edge_scores
+
+            def weighed(scores):
                 top = jnp.max(scores, axis=1, keepdims=True)
                 weights = jnp.exp((scores - top) * scale)
-                total = jnp.sum(weights, axis=1, keepdims=True)
-                summed = jnp.dot(
-                    weights.astype(jnp.bfloat16), values, preferred_element_type=jnp.float32
-                )
+                return weights.astype(jnp.bfloat16), jnp.sum(weights, axis=1, keepdims=True)
+
+            def finished(b, weights, total):
+                values = stacked(2, at, range((b + 1) * step))
+                summed = jnp.dot(weights, values, preferred_element_type=jnp.float32)
                 done = (summed / total).astype(jnp.bfloat16)
                 for k in range(step):
                     token = b * step + k
@@ -256,10 +260,19 @@
                     if h == width // HEAD - 1:
                         copies.append(
                             pltpu.make_async_copy(
-                                held_ref.at[place_out[token]], out_ref.at[place_out[token]], sems.at[token]
+                                held_ref.at[place_out[token]],
+                                out_ref.at[place_out[token]],
+                                sems.at[token],
                             )
                         )
                         copies[-1].start()
+
+            ahead = scored(spans[0])
+            for k, b in enumerate(spans):
+                scores = ahead
+                if k + 1 < len(spans):
+                    ahead = scored(spans[k + 1])
+                finished(b, *weighed(scores))
         for copy in copies:
             copy.wait()
 

time: 46.8 us -> 46.2 us (0.987)
  Pallas kernels: 12 us -> 11.5 us
    pallas_call x1, Pallas kernels: 2.35 us -> 1.82 us  [head_attention(): pl.pallas_call(body, name='head_attention', in_specs=[pl.BlockSpec(memory...]
  transfers between devices with their start and end apart: 4 -> 4, of which waited for: 2 -> 2; matrix products, arithmetic and copies ran while one was open for 4% -> 4% of each run, Pallas kernels for 22% -> 21%
where the time goes in v6:
time: 46.2 us; the launch traced here: 45.8 us
  starting transfers between devices  19.6 us (42%)
  Pallas kernels  11.5 us (25%)
  waiting for transfers between devices  11.2 us (24%)
  other arithmetic  1.8 us (4%)
  local copies, waits for them, and re-layouts  0.87 us (2%)
  between operations  0.76 us (2%)
    all_to_all x2, waiting for transfers between devices, traded(): lax.all_to_all(blocks, 'ctx', 0, 0, tiled=True, axis_index_groups=[list(o...  11.2 us
    all_to_all x2, starting transfers between devices, traded(): lax.all_to_all(blocks, 'ctx', 0, 0, tiled=True, axis_index_groups=[list(o...  10.5 us
    ppermute x2, starting transfers between devices, passed_along(): return lax.ppermute(block, axis, route)  9.09 us
    pallas_call x1, Pallas kernels, hyena_local(): pl.pallas_call(body, name='hyena_local', grid=(width // cols,), in_specs=...  6.88 us
    pallas_call x1, Pallas kernels, head_attention(): pl.pallas_call(body, name='head_attention', in_specs=[pl.BlockSpec(memory...  1.82 us
    pallas_call x1, Pallas kernels, last_rows(): pl.pallas_call(body, name='last_rows', in_specs=[ANYWHERE], out_specs=pl....  1.04 us
    pallas_call x1, Pallas kernels, by_head(): pl.pallas_call(body, name='by_head', in_specs=[pl.BlockSpec(memory_space=...  1.02 us
    convert_element_type x1, other arithmetic, shards(): (gate.astype(jnp.float32) * (part + carried)).astype(jnp.bfloat16)  0.98 us
  transfers between devices with their start and end apart: 4, of which 2 were waited for; matrix products, arithmetic and copies ran while one was open for 4% of the time, Pallas kernels for 21%

profile of v6, /device:TPU:0, one launch (start us, length us, event | category | flops | bytes accessed | tf_op | source)
XLA Modules:
  0.0 45.8 jit_solution(1315981126846821076)
XLA Ops:
  0.6 0.0 copy-start
  0.6 1.0 %last_rows.1 = bf16[56,2048]{1,0:T(8,128)(2,1)S(1)} custom-call(bf16[3,128,2048]{2,1,0:T(8,128)(2,1)} %x_ref.3), custom_call_target="tpu_custom_call" | custom-call | tf_op jit(solution)/shard_map/last_rows/pallas_call | solution.py:89
  1.7 0.0 copy-start.5
  1.7 0.0 copy-start.3
  1.7 5.0 %collective-permute-start = (bf16[56,2048]{1,0:T(8,128)(2,1)S(1)}, bf16[56,2048]{1,0:T(8,128)(2,1)S(1)}, u32[]{:S(2)}, u32[]{:S(2)}) collective-permute-start(bf16[56,2048]{1,0:T(8,128)(2,1)S(1)} %last_rows.1), channel_id=1, source_target_pairs={{0,2},{2,4},{4,6},{6,8},{8,10},{10,12},{12,14},{1,3},{3,5},{5,7},{... | collective-permute-start | bytes 688136 | tf_op jit(solution)/shard_map/ppermute | solution.py:22
  6.7 0.0 copy-done
  6.7 1.0 %by_head.1 = bf16[8,3,128,128]{3,2,1,0:T(8,128)(2,1)} custom-call(bf16[3,128,1024]{2,1,0:T(8,128)(2,1)S(1)} %copy-done), custom_call_target="tpu_custom_call" | custom-call | tf_op jit(solution)/shard_map/by_head/pallas_call | solution.py:57
  7.8 4.9 %all-to-all-start = ((bf16[8,3,128,128]{3,2,1,0:T(8,128)(2,1)}), bf16[8,3,128,128]{3,2,1,0:T(8,128)(2,1)S(1)}, u32[]{:S(2)}, u32[]{:S(2)}) async-start(bf16[8,3,128,128]{3,2,1,0:T(8,128)(2,1)} %by_head.1), calls=%async_computation | async-start | bytes 1572864 | tf_op jit(solution)/shard_map/all_to_all | solution.py:331
  12.7 0.0 copy-done.5
  12.7 0.0 copy-done.3
  12.7 0.1 exponential_multiply_fusion
  12.8 0.1 slice.9
  12.9 0.1 rev.3
  12.9 0.7 %pad_maximum_fusion.filt_ref = f32[128,128]{1,0:T(8,128)} fusion(f32[128,127]{1,0:T(8,128)S(1)} %rev.3, f32[128,1]{1,0:T(8,128)S(1)} %bitcast.2), kind=kLoop, calls=%fused_computation.1 | loop fusion | flops 16384 | bytes 131072 | tf_op jit(solution)/shard_map/concatenate | solution.py:345
  13.7 0.0 collective-permute-done.tail_ref
  13.7 0.0 copy-start.4
  13.7 0.7 %copy-done.4 = bf16[56,2048]{1,0:T(8,128)(2,1)} copy-done((bf16[56,2048]{1,0:T(8,128)(2,1)}, bf16[56,2048]{1,0:T(8,128)(2,1)S(1)}, u32[]{:S(2)}) %copy-start.4) | copy-done | bytes 229400
  14.4 6.9 %hyena_local.1 = (bf16[112,2048]{1,0:T(8,128)(2,1)}, f32[128,2048]{1,0:T(8,128)}, bf16[128,2048]{1,0:T(8,128)(2,1)}) custom-call(bf16[3,128,2048]{2,1,0:T(8,128)(2,1)} %x_ref.3, bf16[56,2048]{1,0:T(8,128)(2,1)} %copy-done.4, f32[3,7,2048]{2,1,0:T(8,128)} %short_ref.1, f32[128,128]{1,0:T(8,128)} %pad_maximum_fusion.filt_ref, f32[1,2048]{1,0:T(1,128)} %bitcast.3), custom_call_target="tpu_custom_call" | custom-call | flops 10737418240 | bytes 3670016 | tf_op jit(solution)/shard_map/hyena_local/pallas_call | solution.py:184
  21.2 0.0 copy-start.1
  21.2 0.0 copy-start.2
  21.3 4.1 %collective-permute-start.1 = (bf16[112,2048]{1,0:T(8,128)(2,1)}, bf16[112,2048]{1,0:T(8,128)(2,1)S(1)}, u32[]{:S(2)}, u32[]{:S(2)}) collective-permute-start(bf16[112,2048]{1,0:T(8,128)(2,1)} %get-tuple-element.7), channel_id=1, source_target_pairs={{0,2},{2,4},{4,6},{6,8},{8,10},{10,12},{12,14},{1,3},{3,5},{5,7},{... | collective-permute-start | bytes 1376264 | tf_op jit(solution)/shard_map/ppermute | solution.py:22
  25.3 4.9 %all-to-all-done.in_ref = bf16[8,3,128,128]{3,2,1,0:T(8,128)(2,1)S(1)} async-done(((bf16[8,3,128,128]{3,2,1,0:T(8,128)(2,1)}), bf16[8,3,128,128]{3,2,1,0:T(8,128)(2,1)S(1)}, u32[]{:S(2)}, u32[]{:S(2)}) %all-to-all-start) | async-done | bytes 786464 | tf_op jit(solution)/shard_map/all_to_all | solution.py:331
  30.3 1.8 %head_attention.1 = bf16[8,128,128]{2,1,0:T(8,128)(2,1)} custom-call(bf16[8,3,128,128]{3,2,1,0:T(8,128)(2,1)S(1)} %all-to-all-done.in_ref), custom_call_target="tpu_custom_call" | custom-call | flops 268435456 | bytes 1048576 | tf_op jit(solution)/shard_map/head_attention/pallas_call | solution.py:280
  32.1 5.7 %all-to-all-start.1 = ((bf16[8,128,128]{2,1,0:T(8,128)(2,1)}), bf16[8,128,128]{2,1,0:T(8,128)(2,1)S(1)}, u32[]{:S(2)}, u32[]{:S(2)}) async-start(bf16[8,128,128]{2,1,0:T(8,128)(2,1)} %head_attention.1), calls=%async_computation.1 | async-start | bytes 524288 | tf_op jit(solution)/shard_map/all_to_all | solution.py:331
  37.8 0.0 collective-permute-done.1
  37.8 0.0 copy-done.1
  37.8 0.0 copy-done.2
  37.8 1.0 %multiply_convert_fusion = bf16[128,2048]{1,0:T(8,128)(2,1)} fusion(f32[128,2048]{1,0:T(8,128)S(1)} %copy-done.1, bf16[128,2048]{1,0:T(8,128)(2,1)S(1)} %copy-done.2, bf16[112,2048]{1,0:T(8,128)(2,1)S(1)} %collective-permute-done.1), kind=kLoop, calls=%fused_computation | loop fusion | flops 1310720 | bytes 2555904 | tf_op jit(solution)/shard_map/convert_element_type | solution.py:354
  38.8 6.3 %all-to-all-done.1.in_ref = bf16[8,128,128]{2,1,0:T(8,128)(2,1)S(1)} async-done(((bf16[8,128,128]{2,1,0:T(8,128)(2,1)}), bf16[8,128,128]{2,1,0:T(8,128)(2,1)S(1)}, u32[]{:S(2)}, u32[]{:S(2)}) %all-to-all-start.1) | async-done | bytes 262176 | tf_op jit(solution)/shard_map/all_to_all | solution.py:331
  45.0 0.8 %by_token.1 = bf16[128,1024]{1,0:T(8,128)(2,1)} custom-call(bf16[8,128,128]{2,1,0:T(8,128)(2,1)S(1)} %all-to-all-done.1.in_ref), custom_call_target="tpu_custom_call" | custom-call | tf_op jit(solution)/shard_map/by_token/pallas_call | solution.py:112
  (1 shorter events, 0.0 us)
Async XLA Ops:
  0.6 6.1 %copy-start = (bf16[3,128,1024]{2,1,0:T(8,128)(2,1)S(1)}, bf16[3,128,1024]{2,1,0:T(8,128)(2,1)}, u32[]{:S(2)}) copy-start(bf16[3,128,1024]{2,1,0:T(8,128)(2,1)} %qkv_ref.1) | copy-start | bytes 2359300
  1.7 11.0 %copy-start.5 = (f32[128]{0:T(128)S(1)}, f32[128]{0:T(128)}, u32[]{:S(2)}) copy-start(f32[128]{0:T(128)} %param.9) | copy-start | bytes 1540
  1.7 11.0 %copy-start.3 = (f32[128,128]{1,0:T(8,128)S(1)}, f32[128,128]{1,0:T(8,128)}, u32[]{:S(2)}) copy-start(f32[128,128]{1,0:T(8,128)} %param.8) | copy-start | bytes 196612
  1.7 12.0 %collective-permute-start = (bf16[56,2048]{1,0:T(8,128)(2,1)S(1)}, bf16[56,2048]{1,0:T(8,128)(2,1)S(1)}, u32[]{:S(2)}, u32[]{:S(2)}) collective-permute-start(bf16[56,2048]{1,0:T(8,128)(2,1)S(1)} %last_rows.1), channel_id=1, source_target_pairs={{0,2},{2,4},{4,6},{6,8},{8,10},{10,12},{12,14},{1,3},{3,5},{5,7},{... | collective-permute-start | bytes 688136 | tf_op jit(solution)/shard_map/ppermute | solution.py:22
  7.8 22.5 %all-to-all-start = ((bf16[8,3,128,128]{3,2,1,0:T(8,128)(2,1)}), bf16[8,3,128,128]{3,2,1,0:T(8,128)(2,1)S(1)}, u32[]{:S(2)}, u32[]{:S(2)}) async-start(bf16[8,3,128,128]{3,2,1,0:T(8,128)(2,1)} %by_head.1), calls=%async_computation | async-start | bytes 1572864 | tf_op jit(solution)/shard_map/all_to_all | solution.py:331
  13.7 0.7 %copy-start.4 = (bf16[56,2048]{1,0:T(8,128)(2,1)}, bf16[56,2048]{1,0:T(8,128)(2,1)S(1)}, u32[]{:S(2)}) copy-start(bf16[56,2048]{1,0:T(8,128)(2,1)S(1)} %collective-permute-done.tail_ref) | copy-start | bytes 688132
  21.2 16.5 %copy-start.1 = (f32[128,2048]{1,0:T(8,128)S(1)}, f32[128,2048]{1,0:T(8,128)}, u32[]{:S(2)}) copy-start(f32[128,2048]{1,0:T(8,128)} %get-tuple-element.6) | copy-start | bytes 3145732
  21.2 16.5 %copy-start.2 = (bf16[128,2048]{1,0:T(8,128)(2,1)S(1)}, bf16[128,2048]{1,0:T(8,128)(2,1)}, u32[]{:S(2)}) copy-start(bf16[128,2048]{1,0:T(8,128)(2,1)} %get-tuple-element.5) | copy-start | bytes 1572868
  21.3 16.5 %collective-permute-start.1 = (bf16[112,2048]{1,0:T(8,128)(2,1)}, bf16[112,2048]{1,0:T(8,128)(2,1)S(1)}, u32[]{:S(2)}, u32[]{:S(2)}) collective-permute-start(bf16[112,2048]{1,0:T(8,128)(2,1)} %get-tuple-element.7), channel_id=1, source_target_pairs={{0,2},{2,4},{4,6},{6,8},{8,10},{10,12},{12,14},{1,3},{3,5},{5,7},{... | collective-permute-start | bytes 1376264 | tf_op jit(solution)/shard_map/ppermute | solution.py:22
  32.1 12.9 %all-to-all-start.1 = ((bf16[8,128,128]{2,1,0:T(8,128)(2,1)}), bf16[8,128,128]{2,1,0:T(8,128)(2,1)S(1)}, u32[]{:S(2)}, u32[]{:S(2)}) async-start(bf16[8,128,128]{2,1,0:T(8,128)(2,1)} %head_attention.1), calls=%async_computation.1 | async-start | bytes 524288 | tf_op jit(solution)/shard_map/all_to_all | solution.py:331
